TPU v7x, 32 devices: a whole 2x2x4 slice. The times are simulated.
32 devices in a mesh: user: 8 (over y, x, core), item: 4 (over z).
Axes of the slice: x: 2, y: 2, z: 4, core: 2. Of those that a mesh axis runs over, the one named last changes fastest.
Arguments:
- tokens: bfloat16 [16384, 1024], P(('user', 'item')), may hold values from -6 to 6
- lengths: int32 [32, 8], P(('user', 'item')), may hold values from 1 to 64, as said below
- destination: int32 [32, 8], P(('user', 'item')), may hold values from 0 to 7, as said below
- worker_offset: int32 [32, 8], P(('user', 'item')), may hold values from 0 to 255
- positives: int32 [16384], P(('user', 'item')), may hold values from 0 to 1023, as said below
- negatives: int32 [4, 256], replicated, may hold values from 0 to 1023, as said below
- table: bfloat16 [1024, 1024], P('item'), may hold values from -6 to 6
- in_gain: float32 [1024], replicated, may hold values from 0.1 to 1.9
- w_uvqk: bfloat16 [1024, 2048], P('item'), may hold values from -0.1875 to 0.1875
- out_gain: float32 [512], replicated, may hold values from 0.1 to 1.9
- w_out: bfloat16 [512, 1024], P(None, 'item'), may hold values from -0.25 to 0.25
Outputs:
- layer_out: bfloat16 [8192, 1024], P(('user', 'item'))
- token_grad: bfloat16 [16384, 1024], P(('user', 'item'))
- item_grad: float32 [1024, 1024], P('item', 'user')
Inputs may be any that keep to these rules, and one draw needn't show every extreme that they name: `lengths`: A device's histories lie in its rows in order from row 0 and fill at most 512 rows; every destination receives a history of exactly 64 tokens. `destination`: A device sends its 8 histories to 8 different destinations along user; the histories sent to one device by the devices of its item index, placed at their worker_offset, cover its 256 rows exactly once. `positives`: the target ids of a device lie among the 256 table rows of its item index. `negatives`: columns k * 64 to k * 64 + 63 of each group name rows held by item index k.
All inputs are finite; a program needn't handle non-finite values.
Results may differ from a plain program's by a relative error of at most 0.017.
Values may be sent and summed in bfloat16 or wider, within the bound.
A program may use at most 64 MiB of HBM per device.

v0:
```python
import jax
import jax.numpy as jnp
from jax import lax
from jax.sharding import PartitionSpec as P

HEAD = 128
TOK_DEV = 256


norm_epsilon = 1e-05
scale_epsilon = 1e-06
inverse_temp = 20.0
loss_scale = 32.0


def layer_norm(values, gain):
    center = jnp.mean(values, axis=-1, keepdims=True)
    shifted = values - center
    spread = jnp.mean(shifted * shifted, axis=-1, keepdims=True)
    return shifted * lax.rsqrt(spread + norm_epsilon) * gain


def hstu_block(rows, segment, in_gain, w_uvqk, out_gain, w_out):
    count = rows.shape[0]
    rows_f = rows.astype(jnp.float32)
    normed = layer_norm(rows_f, in_gain).astype(jnp.bfloat16)
    projected = jnp.dot(
        normed,
        lax.all_gather(w_uvqk, "item", axis=0, tiled=True),
        preferred_element_type=jnp.float32,
    )
    active = jax.nn.silu(projected).astype(jnp.bfloat16)
    width = active.shape[1] // 4
    heads = width // HEAD
    gate_u = active[:, :width]
    values_v = active[:, width : 2 * width].reshape(count, heads, HEAD)
    queries = active[:, 2 * width : 3 * width].reshape(count, heads, HEAD)
    key_rows = active[:, 3 * width :].reshape(count, heads, HEAD)
    scores = jnp.einsum(
        "qhd,khd->hqk", queries, key_rows, preferred_element_type=jnp.float32
    ) * HEAD ** (-0.5)
    order = jnp.arange(count, dtype=jnp.int32)
    allowed = (segment[:, None] == segment[None, :]) & (order[None, :] <= order[:, None])
    weights = jnp.where(allowed[None], jax.nn.silu(scores), 0.0).astype(jnp.bfloat16)
    mixed = jnp.einsum(
        "hqk,khd->qhd", weights, values_v, preferred_element_type=jnp.float32
    ).reshape(count, width)
    gated = (layer_norm(mixed, out_gain) * gate_u.astype(jnp.float32)).astype(jnp.bfloat16)
    delta = jnp.dot(
        gated, lax.all_gather(w_out, "item", axis=1, tiled=True), preferred_element_type=jnp.float32
    )
    return (rows_f + delta).astype(jnp.bfloat16)


def dispatch(rows, home_start, history_len, targets, offsets, slot_rows, user_count):
    peers = jnp.arange(user_count, dtype=jnp.int32)
    chosen = (targets[None, :] == peers[:, None]).astype(jnp.int32)
    first_row = jnp.sum(chosen * home_start[None, :], axis=1)
    sent_count = jnp.sum(chosen * history_len[None, :], axis=1)
    landing = jnp.sum(chosen * offsets[None, :], axis=1)
    within = jnp.arange(slot_rows, dtype=jnp.int32)
    picked = jnp.minimum(first_row[:, None] + within[None, :], rows.shape[0] - 1)
    filled = within[None, :] < sent_count[:, None]
    parcels = jnp.where(filled[:, :, None], rows[picked], jnp.zeros((), rows.dtype))
    labels = jnp.stack([landing, sent_count], axis=1)
    arrived, arrived_labels = (
        lax.all_to_all(parcels, "user", split_axis=0, concat_axis=0, tiled=True),
        lax.all_to_all(labels, "user", split_axis=0, concat_axis=0, tiled=True),
    )
    worker_rows = jnp.arange(TOK_DEV, dtype=jnp.int32)
    lower = arrived_labels[:, 0]
    upper = lower + arrived_labels[:, 1]
    inside = (
        (worker_rows[:, None] >= lower[None, :]) & (worker_rows[:, None] < upper[None, :])
    ).astype(jnp.int32)
    source = jnp.sum(inside * peers[None, :], axis=1)
    begin = jnp.sum(inside * lower[None, :], axis=1)
    flattened = arrived.reshape(-1, arrived.shape[-1])
    gathered = flattened[source * slot_rows + worker_rows - begin]
    return (gathered, source, arrived_labels)


def per_device(
    tokens,
    lengths,
    destination,
    worker_offset,
    positives,
    negatives,
    table,
    in_gain,
    w_uvqk,
    out_gain,
    w_out,
):
    user_count = lax.axis_size("user")
    item_count = lax.axis_size("item")
    item_here = lax.axis_index("item")
    user_here = lax.axis_index("user")
    home_rows = tokens.shape[0]
    model_width = tokens.shape[1]
    hist_count = lengths.shape[1]
    slot_rows = home_rows // hist_count
    history_len = lengths[0]
    targets = destination[0]
    offsets = worker_offset[0]
    home_start = jnp.cumsum(history_len) - history_len
    row_ids = jnp.arange(home_rows, dtype=jnp.int32)
    finished = (row_ids[:, None] >= (home_start + history_len)[None, :]).astype(jnp.int32)
    home_segment = jnp.sum(finished, axis=1)
    valid = row_ids < jnp.sum(history_len)
    home_out = hstu_block(tokens, home_segment, in_gain, w_uvqk, out_gain, w_out)
    layer_out = dispatch(
        home_out, home_start, history_len, targets, offsets, slot_rows, user_count
    )[0]
    item_rows = table.shape[0]
    table_f = table.astype(jnp.float32)
    table_scale = lax.rsqrt(jnp.mean(table_f * table_f, axis=1) + scale_epsilon)
    table_hat = table_f * table_scale[:, None]
    table_low = table_hat.astype(jnp.bfloat16)
    share = negatives.shape[1] // item_count
    owned_ids = (
        lax.dynamic_slice_in_dim(negatives, item_here * share, share, 1) - item_here * item_rows
    )
    group_rows = lax.all_to_all(
        table_low[owned_ids], "item", split_axis=0, concat_axis=0, tiled=True
    ).reshape(-1, model_width)
    positive_local = positives - item_here * item_rows
    positive_rows = table_low[positive_local]
    out_f = home_out.astype(jnp.float32)
    out_scale = lax.rsqrt(jnp.mean(out_f * out_f, axis=1) + scale_epsilon)
    out_hat = out_f * out_scale[:, None]
    out_low = out_hat.astype(jnp.bfloat16)
    factor = inverse_temp / model_width
    positive_logit = (
        jnp.einsum("rd,rd->r", out_low, positive_rows, preferred_element_type=jnp.float32) * factor
    )
    negative_logit = (
        jnp.einsum("rd,nd->rn", out_low, group_rows, preferred_element_type=jnp.float32) * factor
    )
    positive_exp = jnp.exp(positive_logit)
    negative_exp = jnp.exp(negative_logit)
    partition = positive_exp + jnp.sum(negative_exp, axis=1)
    weight = jnp.where(valid, loss_scale, 0.0)
    positive_grad = weight * (positive_exp / partition - 1.0)
    negative_grad = (weight[:, None] * negative_exp / partition[:, None]).astype(jnp.bfloat16)
    grad_hat = (
        positive_grad[:, None] * positive_rows.astype(jnp.float32)
        + jnp.dot(negative_grad, group_rows, preferred_element_type=jnp.float32)
    ) * factor
    token_grad = (
        (grad_hat - out_hat * jnp.mean(grad_hat * out_hat, axis=1, keepdims=True))
        * out_scale[:, None]
    ).astype(jnp.bfloat16)
    negative_terms = (
        jnp.einsum("rn,rd->nd", negative_grad, out_low, preferred_element_type=jnp.float32) * factor
    )
    owned_terms = lax.all_to_all(
        negative_terms.reshape(item_count, share, model_width).astype(jnp.bfloat16),
        "item",
        split_axis=0,
        concat_axis=0,
        tiled=True,
    ).astype(jnp.float32)
    positive_terms = (positive_grad * factor)[:, None] * out_low.astype(jnp.float32)
    catalog = jnp.arange(item_rows, dtype=jnp.int32)
    positive_hits = (positive_local[None, :] == catalog[:, None]).astype(jnp.float32)
    negative_hits = (owned_ids.reshape(-1)[None, :] == catalog[:, None]).astype(jnp.float32)
    row_sums = jnp.dot(positive_hits, positive_terms, precision=lax.Precision.HIGHEST)
    row_sums = row_sums + jnp.dot(
        negative_hits, owned_terms.reshape(-1, model_width), precision=lax.Precision.HIGHEST
    )
    column_width = model_width // user_count
    totals = lax.psum(row_sums.astype(jnp.bfloat16), "user").astype(jnp.float32)
    inner = jnp.mean(totals * table_hat, axis=1)
    whole = (totals - table_hat * inner[:, None]) * table_scale[:, None]
    item_grad = lax.dynamic_slice_in_dim(whole, user_here * column_width, column_width, 1)
    return (layer_out, token_grad, item_grad)


def solution(mesh):
    return jax.shard_map(
        per_device,
        mesh=mesh,
        in_specs=(
            P(("user", "item"), None),
            P(("user", "item"), None),
            P(("user", "item"), None),
            P(("user", "item"), None),
            P(("user", "item")),
            P(),
            P("item", None),
            P(),
            P("item", None),
            P(),
            P(None, "item"),
        ),
        out_specs=(P(("user", "item"), None), P(("user", "item"), None), P("item", "user")),
        check_vma=False,
    )
```

profile of v0, /device:TPU:9, one launch (start us, length us, event | category | flops | bytes accessed | tf_op | source)
XLA Modules:
  0.0 227.0 jit_solution(2644495984975450326)
XLA Ops:
  7.9 0.8 reduce-window.4
  8.8 1.4 fusion.62
  10.1 0.8 select_reduce_fusion.2
  11.7 4.4 %all-to-all-start.1 = ((s32[8,1,2]{2,1,0:T(1,128)}), s32[8,1,2]{2,1,0:T(1,128)S(1)}, u32[]{:S(2)}, u32[]{:S(2)}) async-start(s32[8,1,2]{2,1,0:T(1,128)} %copy.32), calls=%async_computation.1 | async-start | bytes 8192 | tf_op jit(solution)/shard_map/all_to_all | solution.py:68
  16.1 0.7 all-gather.5.cloned.1.call-update
  16.9 1.5 convert_reduce_fusion
  19.7 2.0 gather_fusion.2
  21.8 2.0 gather_fusion.3
  24.7 4.8 %all-to-all-start.2 = ((bf16[4,64,1024]{2,1,0:T(8,128)(2,1)}), bf16[4,64,1024]{2,1,0:T(8,128)(2,1)S(1)}, u32[]{:S(2)}, u32[]{:S(2)}) async-start(bf16[4,64,1024]{2,1,0:T(8,128)(2,1)} %bitcast.67), calls=%async_computation.2 | async-start | bytes 1048576 | tf_op jit(solution)/shard_map/all_to_all | solution.py:125
  29.7 69.3 %all-gather.3.cloned.1.call-done = bf16[1024,2048]{1,0:T(8,128)(2,1)} async-done(((bf16[256,2048]{1,0:T(8,128)(2,1)}), bf16[1024,2048]{1,0:T(8,128)(2,1)}) %all-gather.3.cloned.1.call-update) | async-done | bytes 4194320 | tf_op jit(solution)/shard_map/all_gather | solution.py:29
  99.0 5.1 %multiply_convert_fusion = bf16[512,2048]{1,0:T(8,128)(2,1)S(1)} fusion(bf16[1024,2048]{1,0:T(8,128)(2,1)} %all-gather.3.cloned.1.call-done, bf16[512,1024]{1,0:T(8,128)(2,1)S(1)} %copy-done.1, f32[1024]{0:T(1024)S(1)} %copy-done.8, f32[512]{0:T(512)S(1)} %add_rsqrt_fusion.2, f32[512]{0:T(512)S(1)} %broadcast_multiply_fusion.3), kind=kOutput, calls=%fused_computation.5 | convolution fusion | flops 2155347968 | bytes 7348224 | tf_op jit(solution)/shard_map/dot_general | solution.py:27
  104.1 1.3 copy-done.3
  105.4 1.2 slice_bitcast_fusion.1
  106.6 1.0 copy.38
  107.6 3.4 %fusion.63 = (f32[512]{0:T(512)S(1)}, f32[4,128,512]{2,1,0:T(8,128)S(1)}) fusion(bf16[512,4,128]{0,2,1:T(8,128)(2,1)} %bitcast.72, pred[512,512]{1,0:T(8,128)(4,1)S(1)} %fusion.34, bf16[64,4,8,128]{3,2,1,0:T(8,128)(2,1)} %get-tuple-element.15, bf16[64,4,8,128]{3,2,1,0:T(8,128)(2,1)} %get-tuple-element.14), kind=kOutput, calls=%fused_computation.121 | convolution fusion | flops 544472576 | bytes 2885632 | tf_op jit(solution)/shard_map/hqk,khd->qhd/dot_general | solution.py:45
  111.0 1.3 copy.39
  112.5 16.7 %all-gather.5.cloned.1.call-done = bf16[512,1024]{1,0:T(8,128)(2,1)} async-done(((bf16[512,256]{1,0:T(8,128)(2,1)}), bf16[512,1024]{1,0:T(8,128)(2,1)}) %all-gather.5.cloned.1.call-update) | async-done | bytes 1048592 | tf_op jit(solution)/shard_map/all_gather | solution.py:50
  129.2 3.0 %fusion.12 = (f32[512]{0:T(512)S(1)}, bf16[512,1024]{1,0:T(8,128)(2,1)S(1)}) fusion(bf16[512,1024]{1,0:T(8,128)(2,1)} %all-gather.5.cloned.1.call-done, f32[512,512]{1,0:T(8,128)} %copy.39, bf16[512,2048]{1,0:T(8,128)(2,1)} %copy-done.3, f32[512]{0:T(512)S(1)} %copy-done.9, f32[512]{0:T(512)S(1)} %add_rsqrt_fusion.1, f32[512]{0:T(512)S(1)} %broadcast_multiply_fusion.1, ...), kind=kOutput, calls=%fused_computation.26 | convolution fusion | flops 541588992 | bytes 4726784 | tf_op jit(solution)/shard_map/dot_general | solution.py:49
  134.1 1.4 fusion.20
  135.4 5.7 %all-to-all-start.3 = ((bf16[4,64,1024]{2,1,0:T(8,128)(2,1)}), bf16[4,64,1024]{2,1,0:T(8,128)(2,1)S(1)}, u32[]{:S(2)}, u32[]{:S(2)}) async-start(bf16[4,64,1024]{2,1,0:T(8,128)(2,1)} %bitcast.71), calls=%async_computation.3 | async-start | bytes 1048576 | tf_op jit(solution)/shard_map/all_to_all | solution.py:158
  141.2 2.8 %gather_fusion = bf16[512,1024]{1,0:T(8,128)(2,1)} fusion(bf16[512,1024]{1,0:T(8,128)(2,1)S(1)} %get-tuple-element.25, s32[1024]{0:T(1024)S(1)} %pad_clamp_fusion.3), kind=kCustom, calls=%fused_computation | custom fusion | bytes 2099200 | tf_op jit(solution)/shard_map/gather | solution.py:64
  144.0 2.4 %broadcast_select_fusion = bf16[8,64,1024]{2,1,0:T(8,128)(2,1)} fusion(bf16[8,64,1024]{2,1,0:T(8,128)(2,1)} %bitcast.65, pred[8,64]{1,0:T(8,128)(4,1)S(1)} %iota_compare_fusion.9), kind=kLoop, calls=%fused_computation.54 | loop fusion | flops 524288 | bytes 2097664 | tf_op jit(solution)/shard_map/jit(_where)/select_n | solution.py:64
  146.4 2.1 fusion.8
  148.5 2.9 %all-to-all-done.3 = bf16[4,64,1024]{2,1,0:T(8,128)(2,1)S(1)} async-done(((bf16[4,64,1024]{2,1,0:T(8,128)(2,1)}), bf16[4,64,1024]{2,1,0:T(8,128)(2,1)S(1)}, u32[]{:S(2)}, u32[]{:S(2)}) %all-to-all-start.3) | async-done | bytes 524320 | tf_op jit(solution)/shard_map/all_to_all | solution.py:158
  151.4 6.5 %all-to-all-start = ((bf16[8,64,1024]{2,1,0:T(8,128)(2,1)}), bf16[8,64,1024]{2,1,0:T(8,128)(2,1)S(1)}, u32[]{:S(2)}, u32[]{:S(2)}) async-start(bf16[8,64,1024]{2,1,0:T(8,128)(2,1)} %broadcast_select_fusion), calls=%async_computation | async-start | bytes 2097152 | tf_op jit(solution)/shard_map/all_to_all | solution.py:67
  158.2 2.4 %fusion.21 = bf16[256,1024]{1,0:T(8,128)(2,1)} fusion(f32[256,1024]{1,0:T(8,128)S(1)} %fusion.48, f32[512]{0:T(512)S(1)} %get-tuple-element.8, s32[512]{0:T(512)S(1)} %get-tuple-element.13, bf16[512,1024]{1,0:T(8,128)(2,1)S(1)} %get-tuple-element.25, f32[512]{0:T(512)S(1)} %add_rsqrt_fusion), kind=kOutput, calls=%fused_computation.38 | convolution fusion | flops 1613889536 | bytes 2627584 | tf_op jit(solution)/shard_map/dot_general | solution.py:169
  160.6 3.0 %fusion.11 = bf16[512,1024]{1,0:T(8,128)(2,1)} fusion(f32[512,1024]{1,0:T(8,128)} %get-tuple-element.29, bf16[512,1024]{1,0:T(8,128)(2,1)S(1)} %get-tuple-element.25, f32[512]{0:T(512)S(1)} %broadcast_multiply_fusion.2, f32[512]{0:T(512)S(1)} %add_rsqrt_fusion), kind=kLoop, calls=%fused_computation.25 | loop fusion | flops 3145728 | bytes 4198400 | tf_op jit(solution)/shard_map/convert_element_type | solution.py:154
  163.6 6.8 %all-to-all-done = bf16[8,64,1024]{2,1,0:T(8,128)(2,1)S(1)} async-done(((bf16[8,64,1024]{2,1,0:T(8,128)(2,1)}), bf16[8,64,1024]{2,1,0:T(8,128)(2,1)S(1)}, u32[]{:S(2)}, u32[]{:S(2)}) %all-to-all-start) | async-done | bytes 1048608 | tf_op jit(solution)/shard_map/all_to_all | solution.py:67
  170.4 2.0 gather_fusion.1
  172.3 45.8 %all-reduce.2.cloned.1.call-done = bf16[256,1024]{1,0:T(8,128)(2,1)} async-done(((bf16[256,1024]{1,0:T(8,128)(2,1)}), bf16[256,1024]{1,0:T(8,128)(2,1)}) %all-reduce.2.cloned.1.call-update) | async-done | bytes 524304 | tf_op jit(solution)/shard_map/psum | solution.py:174
  218.1 1.4 multiply_reduce_fusion
  219.7 0.8 fusion.49
  (69 shorter events, 6.4 us)
Async XLA Ops:
  7.2 11.2 %copy-start.1 = (bf16[512,1024]{1,0:T(8,128)(2,1)S(1)}, bf16[512,1024]{1,0:T(8,128)(2,1)}, u32[]{:S(2)}) copy-start(bf16[512,1024]{1,0:T(8,128)(2,1)} %param.11) | copy-start | bytes 3145732
  7.2 12.0 %copy-start.6 = (s32[512]{0:T(512)S(1)}, s32[512]{0:T(512)}, u32[]{:S(2)}) copy-start(s32[512]{0:T(512)} %param.15) | copy-start | bytes 6148
  7.2 12.0 %copy-start = (bf16[256,1024]{1,0:T(8,128)(2,1)S(1)}, bf16[256,1024]{1,0:T(8,128)(2,1)}, u32[]{:S(2)}) copy-start(bf16[256,1024]{1,0:T(8,128)(2,1)} %param.17) | copy-start | bytes 1572868
  7.2 91.8 %all-gather.3.cloned.1.call-start = ((), (), s32[]{:S(2)}) async-start(), calls=%async_computation.4 | async-start | bytes 5242880 | tf_op jit(solution)/shard_map/all_gather | solution.py:29
  11.7 13.1 %all-to-all-start.1 = ((s32[8,1,2]{2,1,0:T(1,128)}), s32[8,1,2]{2,1,0:T(1,128)S(1)}, u32[]{:S(2)}, u32[]{:S(2)}) async-start(s32[8,1,2]{2,1,0:T(1,128)} %copy.32), calls=%async_computation.1 | async-start | bytes 8192 | tf_op jit(solution)/shard_map/all_to_all | solution.py:68
  16.1 3.5 %copy-start.7 = (s32[4,256]{1,0:T(4,128)S(1)}, s32[4,256]{1,0:T(4,128)}, u32[]{:S(2)}) copy-start(s32[4,256]{1,0:T(4,128)} %param.16) | copy-start | bytes 12292
  16.1 113.2 %all-gather.5.cloned.1.call-start = ((), (), s32[]{:S(2)}) async-start(), calls=%async_computation.5 | async-start | bytes 1310720 | tf_op jit(solution)/shard_map/all_gather | solution.py:50
  21.8 77.2 %copy-start.8 = (f32[1024]{0:T(1024)S(1)}, f32[1024]{0:T(1024)}, u32[]{:S(2)}) copy-start(f32[1024]{0:T(1024)} %param.18) | copy-start | bytes 12292
  24.7 108.0 %all-to-all-start.2 = ((bf16[4,64,1024]{2,1,0:T(8,128)(2,1)}), bf16[4,64,1024]{2,1,0:T(8,128)(2,1)S(1)}, u32[]{:S(2)}, u32[]{:S(2)}) async-start(bf16[4,64,1024]{2,1,0:T(8,128)(2,1)} %bitcast.67), calls=%async_computation.2 | async-start | bytes 1048576 | tf_op jit(solution)/shard_map/all_to_all | solution.py:125
  104.1 1.4 copy-start.3
  111.0 18.2 %copy-start.9 = (f32[512]{0:T(512)S(1)}, f32[512]{0:T(512)}, u32[]{:S(2)}) copy-start(f32[512]{0:T(512)} %param.20) | copy-start | bytes 6148
  132.7 2.7 %copy-start.4 = (bf16[4,64,1024]{2,1,0:T(8,128)(2,1)}, bf16[4,64,1024]{2,1,0:T(8,128)(2,1)S(1)}, u32[]{:S(2)}) copy-start(bf16[4,64,1024]{2,1,0:T(8,128)(2,1)S(1)} %all-to-all-done.2) | copy-start | bytes 1572868
  133.3 0.8 copy-start.10
  135.4 16.0 %all-to-all-start.3 = ((bf16[4,64,1024]{2,1,0:T(8,128)(2,1)}), bf16[4,64,1024]{2,1,0:T(8,128)(2,1)S(1)}, u32[]{:S(2)}, u32[]{:S(2)}) async-start(bf16[4,64,1024]{2,1,0:T(8,128)(2,1)} %bitcast.71), calls=%async_computation.3 | async-start | bytes 1048576 | tf_op jit(solution)/shard_map/all_to_all | solution.py:158
  143.9 2.4 %copy-start.5 = (bf16[4,64,1024]{2,1,0:T(8,128)(2,1)S(1)}, bf16[4,64,1024]{2,1,0:T(8,128)(2,1)}, u32[]{:S(2)}) copy-start(bf16[4,64,1024]{2,1,0:T(8,128)(2,1)} %copy-done.4) | copy-start | bytes 1572868
  143.9 2.4 %copy-start.11 = (f32[512,256]{0,1:T(8,128)S(1)}, f32[512,256]{0,1:T(8,128)}, u32[]{:S(2)}) copy-start(f32[512,256]{0,1:T(8,128)} %copy-done.10) | copy-start | bytes 1572868
  151.4 19.0 %all-to-all-start = ((bf16[8,64,1024]{2,1,0:T(8,128)(2,1)}), bf16[8,64,1024]{2,1,0:T(8,128)(2,1)S(1)}, u32[]{:S(2)}, u32[]{:S(2)}) async-start(bf16[8,64,1024]{2,1,0:T(8,128)(2,1)} %broadcast_select_fusion), calls=%async_computation | async-start | bytes 2097152 | tf_op jit(solution)/shard_map/all_to_all | solution.py:67
  157.9 60.2 %all-reduce.2.cloned.1.call-start = ((), (), s32[]{:S(2)}) async-start(), calls=%async_computation.6 | async-start | bytes 1048576 | tf_op jit(solution)/shard_map/psum | solution.py:174
  218.1 1.4 copy-start.2
Sparse Core Ops, SparseCore 0:
  9.6 89.3 all-gather.2
  100.5 28.6 all-gather.4
  161.8 56.2 all-reduce.1
where the time goes:
time: 230 us; the launch traced here: 227 us
  waiting for transfers between devices  143 us (62%)
  starting transfers between devices  21.4 us (9%)
  matrix products  18.1 us (8%)
  other arithmetic  15.9 us (7%)
  local copies, waits for them, and re-layouts  14.7 us (6%)
  between operations  14 us (6%)
    all_gather x1, waiting for transfers between devices, hstu_block(): lax.all_gather(w_uvqk, 'item', axis=0, tiled=True)  69.3 us
    psum x1, waiting for transfers between devices, per_device(): totals = lax.psum(row_sums.astype(jnp.bfloat16), 'user').astype(jnp.float32)  45.8 us
    all_gather x1, waiting for transfers between devices, hstu_block(): lax.all_gather(w_out, 'item', axis=1, tiled=True)  16.7 us
    all_to_all x1, waiting for transfers between devices, dispatch(): lax.all_to_all(parcels, 'user', split_axis=0, concat_axis=0, tiled=True)  6.77 us
    all_to_all x1, starting transfers between devices, dispatch(): lax.all_to_all(parcels, 'user', split_axis=0, concat_axis=0, tiled=True)  6.46 us
    all_to_all x1, starting transfers between devices, per_device(): lax.all_to_all(negative_terms.reshape(item_count, share, model_width).ast...  5.71 us
    dot_general x1, matrix products, hstu_block(): jnp.dot(normed, lax.all_gather(w_uvqk, 'item', axis=0, tiled=True), prefe...  5.07 us
    all_to_all x1, starting transfers between devices, per_device(): lax.all_to_all(table_low[owned_ids], 'item', split_axis=0, concat_axis=0,...  4.77 us
  transfers between devices with their start and end apart: 7, of which 5 were waited for; matrix products, arithmetic and copies ran while one was open for 19% of the time, Pallas kernels for 0%

commit v1 on v0

--- a/solution.py
+++ b/solution.py
@@ -1,6 +1,10 @@
+import functools
+
 import jax
 import jax.numpy as jnp
 from jax import lax
+from jax.experimental import pallas as pl
+from jax.experimental.pallas import tpu as pltpu
 from jax.sharding import PartitionSpec as P
 
 HEAD = 128
@@ -178,9 +182,392 @@
     return (layer_out, token_grad, item_grad)
 
 
+MESH = pl.DeviceIdType.MESH
+VMEM_SPEC = pl.BlockSpec(memory_space=pltpu.VMEM)
+
+
+def remote(src, dst, send_sem, recv_sem, user, item):
+    return pltpu.make_async_remote_copy(
+        src_ref=src,
+        dst_ref=dst,
+        send_sem=send_sem,
+        recv_sem=recv_sem,
+        device_id=(user, item),
+        device_id_type=MESH,
+    )
+
+
+def greet(users, items, u, i):
+    barrier = pltpu.get_barrier_semaphore()
+    for d in range(1, users):
+        pl.semaphore_signal(
+            barrier, inc=1, device_id=(lax.rem(u + d, users), i), device_id_type=MESH
+        )
+    for d in range(1, items):
+        pl.semaphore_signal(
+            barrier, inc=1, device_id=(u, lax.rem(i + d, items)), device_id_type=MESH
+        )
+    pl.semaphore_wait(barrier, users + items - 2)
+
+
+def gather_kernel(
+    users, items, w_ref, o_ref, n_ref, l_ref, wf, of, nf, lf,
+    own_sem, s1, r1, s2, r2, s3, r3, sn, rn, sl, rl,
+):
+    u = lax.axis_index("user")
+    i = lax.axis_index("item")
+    sibling = u + 1 - 2 * lax.rem(u, 2)
+    half = users // 2
+    greet(users, items, u, i)
+    pairs = ((w_ref, wf), (o_ref, of))
+    sent = []
+    for a, (src, dst) in enumerate(pairs):
+        for d in range(1, items):
+            c = remote(src.at[u], dst.at[i, u], s1.at[a, d - 1], r1.at[a, d - 1], u, lax.rem(i + d, items))
+            c.start()
+            sent.append(c)
+    for d in range(1, users):
+        u2 = lax.rem(u + d, users)
+        c = remote(l_ref.at[u2], lf.at[u], sl.at[d - 1], rl.at[d - 1], u2, i)
+        c.start()
+        sent.append(c)
+    for d in range(1, items):
+        i2 = lax.rem(i + d, items)
+        c = remote(n_ref.at[i2], nf.at[i], sn.at[d - 1], rn.at[d - 1], u, i2)
+        c.start()
+        sent.append(c)
+    local = [
+        pltpu.make_async_copy(w_ref, wf.at[i], own_sem.at[0]),
+        pltpu.make_async_copy(o_ref, of.at[i], own_sem.at[1]),
+        pltpu.make_async_copy(n_ref.at[i], nf.at[i], own_sem.at[2]),
+        pltpu.make_async_copy(l_ref.at[u], lf.at[u], own_sem.at[3]),
+    ]
+    for c in local:
+        c.start()
+    for a, (src, dst) in enumerate(pairs):
+        for d in range(1, items):
+            i2 = lax.rem(i + items - d, items)
+            piece = dst.at[i2, u]
+            remote(piece, piece, s1.at[a, d - 1], r1.at[a, d - 1], u, i2).wait_recv()
+            for e in range(1, half):
+                c = remote(piece, piece, s2.at[a, d - 1, e - 1], r2.at[a, d - 1, e - 1], lax.rem(u + 2 * e, users), i)
+                c.start()
+                sent.append(c)
+            c = remote(piece, piece, s3.at[a, d - 1, 0], r3.at[a, d - 1, 0], sibling, i)
+            c.start()
+            sent.append(c)
+    for a, (src, dst) in enumerate(pairs):
+        for d in range(1, items):
+            i2 = lax.rem(i + items - d, items)
+            for e in range(1, half):
+                u2 = lax.rem(u + users - 2 * e, users)
+                piece = dst.at[i2, u2]
+                remote(piece, piece, s2.at[a, d - 1, e - 1], r2.at[a, d - 1, e - 1], u2, i).wait_recv()
+                c = remote(piece, piece, s3.at[a, d - 1, e], r3.at[a, d - 1, e], sibling, i)
+                c.start()
+                sent.append(c)
+    for a, (src, dst) in enumerate(pairs):
+        for d in range(1, items):
+            i2 = lax.rem(i + items - d, items)
+            for e in range(half):
+                piece = dst.at[i2, lax.rem(sibling + users - 2 * e, users)]
+                remote(piece, piece, s3.at[a, d - 1, e], r3.at[a, d - 1, e], sibling, i).wait_recv()
+    for d in range(1, items):
+        i2 = lax.rem(i + items - d, items)
+        remote(nf.at[i2], nf.at[i2], sn.at[d - 1], rn.at[d - 1], u, i2).wait_recv()
+    for d in range(1, users):
+        u2 = lax.rem(u + users - d, users)
+        remote(lf.at[u2], lf.at[u2], sl.at[d - 1], rl.at[d - 1], u2, i).wait_recv()
+    for c in local:
+        c.wait()
+    for c in sent:
+        c.wait_send()
+
+
+def gather_all(users, items, w, w_o, rows, labels):
+    dma = pltpu.SemaphoreType.DMA
+    half = users // 2
+    w3 = w.reshape(users, w.shape[0] // users, w.shape[1])
+    o3 = w_o.reshape(users, w_o.shape[0] // users, w_o.shape[1])
+    return pl.pallas_call(
+        functools.partial(gather_kernel, users, items),
+        out_shape=(
+            jax.ShapeDtypeStruct((items,) + w3.shape, w.dtype),
+            jax.ShapeDtypeStruct((items,) + o3.shape, w_o.dtype),
+            jax.ShapeDtypeStruct(rows.shape, rows.dtype),
+            jax.ShapeDtypeStruct(labels.shape, labels.dtype),
+        ),
+        in_specs=[VMEM_SPEC] * 4,
+        out_specs=(VMEM_SPEC,) * 4,
+        scratch_shapes=[
+            dma((4,)),
+            dma((2, items - 1)), dma((2, items - 1)),
+            dma((2, items - 1, half - 1)), dma((2, items - 1, half - 1)),
+            dma((2, items - 1, half)), dma((2, items - 1, half)),
+            dma((items - 1,)), dma((items - 1,)),
+            dma((users - 1,)), dma((users - 1,)),
+        ],
+        compiler_params=pltpu.CompilerParams(collective_id=0, has_side_effects=True),
+    )(w3, o3, rows, labels)
+
+
+def tail_kernel(
+    users, items, parcels, terms, pos_sums, neg_hits, place, table_hat, table_scale,
+    layer_out, item_grad,
+    arrived, owned, chunks, got, inner_out, inner_got,
+    own_sem, sd, rd, sn, rn, sc, rc, si, ri,
+):
+    u = lax.axis_index("user")
+    i = lax.axis_index("item")
+    width = layer_out.shape[1]
+    cols = width // users
+    greet(users, items, u, i)
+    sent = []
+    for d in range(1, items):
+        i2 = lax.rem(i + d, items)
+        c = remote(terms.at[i2], owned.at[i], sn.at[d - 1], rn.at[d - 1], u, i2)
+        c.start()
+        sent.append(c)
+    for d in range(1, users):
+        u2 = lax.rem(u + d, users)
+        c = remote(parcels.at[u2], arrived.at[u], sd.at[d - 1], rd.at[d - 1], u2, i)
+        c.start()
+        sent.append(c)
+    local = [
+        pltpu.make_async_copy(terms.at[i], owned.at[i], own_sem.at[0]),
+        pltpu.make_async_copy(parcels.at[u], arrived.at[u], own_sem.at[1]),
+    ]
+    for c in local:
+        c.start()
+    for c in local:
+        c.wait()
+    for d in range(1, items):
+        i2 = lax.rem(i + items - d, items)
+        remote(owned.at[i2], owned.at[i2], sn.at[d - 1], rn.at[d - 1], u, i2).wait_recv()
+    row_sums = pos_sums[...] + jnp.dot(
+        neg_hits[...], owned[...].reshape(-1, width), preferred_element_type=jnp.float32
+    )
+    for v in range(users):
+        chunks[v] = row_sums[:, v * cols : (v + 1) * cols].astype(jnp.bfloat16)
+    inner = jnp.mean(row_sums * table_hat[...], axis=1, keepdims=True)
+    inner_out[...] = jnp.transpose(jnp.broadcast_to(inner, (inner.shape[0], 128)))[:8]
+    for d in range(1, users):
+        u2 = lax.rem(u + d, users)
+        c = remote(chunks.at[u2], got.at[u], sc.at[d - 1], rc.at[d - 1], u2, i)
+        c.start()
+        sent.append(c)
+        c = remote(inner_out, inner_got.at[u], si.at[d - 1], ri.at[d - 1], u2, i)
+        c.start()
+        sent.append(c)
+    total = chunks[u].astype(jnp.float32)
+    inner_total = inner_out[...]
+    for d in range(1, users):
+        u2 = lax.rem(u + users - d, users)
+        remote(arrived.at[u2], arrived.at[u2], sd.at[d - 1], rd.at[d - 1], u2, i).wait_recv()
+    layer_out[...] = jnp.dot(
+        place[...], arrived[...].reshape(-1, width), preferred_element_type=jnp.float32
+    ).astype(jnp.bfloat16)
+    for d in range(1, users):
+        u2 = lax.rem(u + users - d, users)
+        remote(got.at[u2], got.at[u2], sc.at[d - 1], rc.at[d - 1], u2, i).wait_recv()
+        remote(inner_got.at[u2], inner_got.at[u2], si.at[d - 1], ri.at[d - 1], u2, i).wait_recv()
+        total = total + got[u2].astype(jnp.float32)
+        inner_total = inner_total + inner_got[u2]
+    inner_rows = jnp.transpose(jnp.broadcast_to(inner_total[:1], (128, inner_total.shape[1])))
+    here = table_hat[:, pl.ds(pl.multiple_of(u * cols, cols), cols)]
+    item_grad[...] = (total - here * inner_rows[:, :cols]) * table_scale[...]
+    for c in sent:
+        c.wait_send()
+
+
+def tail(users, items, parcels, terms, pos_sums, neg_hits, place, table_hat, table_scale):
+    dma = pltpu.SemaphoreType.DMA
+    width = parcels.shape[-1]
+    cols = width // users
+    count = table_hat.shape[0]
+    return pl.pallas_call(
+        functools.partial(tail_kernel, users, items),
+        out_shape=(
+            jax.ShapeDtypeStruct((place.shape[0], width), jnp.bfloat16),
+            jax.ShapeDtypeStruct((count, cols), jnp.float32),
+        ),
+        in_specs=[VMEM_SPEC] * 7,
+        out_specs=(VMEM_SPEC,) * 2,
+        scratch_shapes=[
+            pltpu.VMEM(parcels.shape, jnp.bfloat16),
+            pltpu.VMEM(terms.shape, jnp.bfloat16),
+            pltpu.VMEM((users, count, cols), jnp.bfloat16),
+            pltpu.VMEM((users, count, cols), jnp.bfloat16),
+            pltpu.VMEM((8, count), jnp.float32),
+            pltpu.VMEM((users, 8, count), jnp.float32),
+            dma((2,)),
+            dma((users - 1,)), dma((users - 1,)),
+            dma((items - 1,)), dma((items - 1,)),
+            dma((users - 1,)), dma((users - 1,)),
+            dma((users - 1,)), dma((users - 1,)),
+        ],
+        compiler_params=pltpu.CompilerParams(collective_id=1, has_side_effects=True),
+    )(parcels, terms, pos_sums, neg_hits, place, table_hat, table_scale)
+
+
+def hstu_whole(rows, segment, in_gain, w_full, out_gain, w_out_full):
+    count = rows.shape[0]
+    rows_f = rows.astype(jnp.float32)
+    normed = layer_norm(rows_f, in_gain).astype(jnp.bfloat16)
+    projected = jnp.dot(normed, w_full, preferred_element_type=jnp.float32)
+    active = jax.nn.silu(projected).astype(jnp.bfloat16)
+    width = active.shape[1] // 4
+    heads = width // HEAD
+    gate_u = active[:, :width]
+    values_v = active[:, width : 2 * width].reshape(count, heads, HEAD)
+    queries = active[:, 2 * width : 3 * width].reshape(count, heads, HEAD)
+    key_rows = active[:, 3 * width :].reshape(count, heads, HEAD)
+    scores = jnp.einsum(
+        "qhd,khd->hqk", queries, key_rows, preferred_element_type=jnp.float32
+    ) * HEAD ** (-0.5)
+    order = jnp.arange(count, dtype=jnp.int32)
+    allowed = (segment[:, None] == segment[None, :]) & (order[None, :] <= order[:, None])
+    weights = jnp.where(allowed[None], jax.nn.silu(scores), 0.0).astype(jnp.bfloat16)
+    mixed = jnp.einsum(
+        "hqk,khd->qhd", weights, values_v, preferred_element_type=jnp.float32
+    ).reshape(count, width)
+    gated = (layer_norm(mixed, out_gain) * gate_u.astype(jnp.float32)).astype(jnp.bfloat16)
+    delta = jnp.concatenate(
+        [jnp.dot(gated, w_out_full[k], preferred_element_type=jnp.float32) for k in range(w_out_full.shape[0])],
+        axis=1,
+    )
+    return (rows_f + delta).astype(jnp.bfloat16)
+
+
+def per_device_kernels(
+    users, items,
+    tokens, lengths, destination, worker_offset, positives, negatives, table,
+    in_gain, w_uvqk, out_gain, w_out,
+):
+    item_here = lax.axis_index("item")
+    home_rows, model_width = tokens.shape
+    slot_rows = home_rows // lengths.shape[1]
+    history_len = lengths[0]
+    targets = destination[0]
+    offsets = worker_offset[0]
+    upto = jnp.arange(lengths.shape[1], dtype=jnp.int32)
+    home_start = jnp.sum(
+        jnp.where(upto[None, :] < upto[:, None], history_len[None, :], 0), axis=1
+    )
+    row_ids = jnp.arange(home_rows, dtype=jnp.int32)
+    finished = (row_ids[:, None] >= (home_start + history_len)[None, :]).astype(jnp.int32)
+    home_segment = jnp.sum(finished, axis=1)
+    valid = row_ids < jnp.sum(history_len)
+    peers = jnp.arange(users, dtype=jnp.int32)
+    chosen = (targets[None, :] == peers[:, None]).astype(jnp.int32)
+    first_row = jnp.sum(chosen * home_start[None, :], axis=1)
+    sent_count = jnp.sum(chosen * history_len[None, :], axis=1)
+    landing = jnp.sum(chosen * offsets[None, :], axis=1)
+    lane = jnp.arange(128, dtype=jnp.int32)
+    labels = jnp.where(lane[None, :] == 0, landing[:, None], sent_count[:, None])
+    labels = jnp.broadcast_to(labels[:, None, :], (users, 8, 128))
+    item_rows = table.shape[0]
+    table_f = table.astype(jnp.float32)
+    table_scale = lax.rsqrt(jnp.mean(table_f * table_f, axis=1) + scale_epsilon)
+    table_hat = table_f * table_scale[:, None]
+    table_low = table_hat.astype(jnp.bfloat16)
+    share = negatives.shape[1] // items
+    owned_ids = (
+        lax.dynamic_slice_in_dim(negatives, item_here * share, share, 1) - item_here * item_rows
+    ).reshape(-1)
+    catalog = jnp.arange(item_rows, dtype=jnp.int32)
+    owned_pick = (owned_ids[:, None] == catalog[None, :]).astype(jnp.bfloat16)
+    owned_rows = jnp.dot(owned_pick, table_low)
+    w_full, w_out_full, group_rows, arrived_labels = gather_all(
+        users, items, w_uvqk, w_out, owned_rows.reshape(items, share, model_width), labels
+    )
+    home_out = hstu_whole(
+        tokens, home_segment, in_gain, w_full.reshape(-1, w_uvqk.shape[1]), out_gain,
+        w_out_full.reshape(items, w_out.shape[0], w_out.shape[1]),
+    )
+    group_rows = group_rows.reshape(-1, model_width)
+    within = jnp.arange(slot_rows, dtype=jnp.int32)
+    wanted = jnp.where(
+        within[None, :] < sent_count[:, None], first_row[:, None] + within[None, :], -1
+    ).reshape(-1)
+    parcel_pick = (wanted[:, None] == row_ids[None, :]).astype(jnp.bfloat16)
+    parcels = jnp.dot(parcel_pick, home_out).reshape(users, slot_rows, model_width)
+    lower = arrived_labels[:, 0, 0]
+    counts = arrived_labels[:, 0, 1]
+    landed = jnp.where(
+        within[None, :] < counts[:, None], lower[:, None] + within[None, :], -1
+    ).reshape(-1)
+    worker_rows = jnp.arange(TOK_DEV, dtype=jnp.int32)
+    place = (landed[None, :] == worker_rows[:, None]).astype(jnp.bfloat16)
+    positive_local = positives - item_here * item_rows
+    positive_pick = positive_local[:, None] == catalog[None, :]
+    positive_rows = jnp.dot(positive_pick.astype(jnp.bfloat16), table_low)
+    out_f = home_out.astype(jnp.float32)
+    out_scale = lax.rsqrt(jnp.mean(out_f * out_f, axis=1) + scale_epsilon)
+    out_hat = out_f * out_scale[:, None]
+    out_low = out_hat.astype(jnp.bfloat16)
+    factor = inverse_temp / model_width
+    positive_logit = (
+        jnp.sum(out_low.astype(jnp.float32) * positive_rows.astype(jnp.float32), axis=1) * factor
+    )
+    negative_logit = (
+        jnp.einsum("rd,nd->rn", out_low, group_rows, preferred_element_type=jnp.float32) * factor
+    )
+    positive_exp = jnp.exp(positive_logit)
+    negative_exp = jnp.exp(negative_logit)
+    partition = positive_exp + jnp.sum(negative_exp, axis=1)
+    weight = jnp.where(valid, loss_scale, 0.0)
+    positive_grad = weight * (positive_exp / partition - 1.0)
+    negative_grad = (weight[:, None] * negative_exp / partition[:, None]).astype(jnp.bfloat16)
+    grad_hat = (
+        positive_grad[:, None] * positive_rows.astype(jnp.float32)
+        + jnp.dot(negative_grad, group_rows, preferred_element_type=jnp.float32)
+    ) * factor
+    token_grad = (
+        (grad_hat - out_hat * jnp.mean(grad_hat * out_hat, axis=1, keepdims=True))
+        * out_scale[:, None]
+    ).astype(jnp.bfloat16)
+    negative_terms = (
+        jnp.einsum("rn,rd->nd", negative_grad, out_low, preferred_element_type=jnp.float32) * factor
+    ).astype(jnp.bfloat16).reshape(items, share, model_width)
+    pos_w = positive_grad * factor
+    pos_hi = pos_w.astype(jnp.bfloat16)
+    pos_lo = (pos_w - pos_hi.astype(jnp.float32)).astype(jnp.bfloat16)
+    zero = jnp.zeros((), jnp.bfloat16)
+    hits_hi = jnp.where(positive_pick, pos_hi[:, None], zero)
+    hits_lo = jnp.where(positive_pick, pos_lo[:, None], zero)
+    pos_sums = jnp.einsum(
+        "rc,rd->cd", hits_hi, out_low, preferred_element_type=jnp.float32
+    ) + jnp.einsum("rc,rd->cd", hits_lo, out_low, preferred_element_type=jnp.float32)
+    neg_hits = (owned_ids[None, :] == catalog[:, None]).astype(jnp.bfloat16)
+    layer_out, item_grad = tail(
+        users, items, parcels, negative_terms, pos_sums, neg_hits, place, table_hat,
+        table_scale[:, None],
+    )
+    return (layer_out, token_grad, item_grad)
+
+
+def step(users, items, tokens, lengths, destination, worker_offset, positives, negatives, table,
+         in_gain, w_uvqk, out_gain, w_out):
+    aligned = (
+        users % 2 == 0
+        and users > 2
+        and items > 1
+        and w_uvqk.shape[0] % (16 * users) == 0
+        and w_out.shape[0] % (16 * users) == 0
+        and w_out.shape[1] % 128 == 0
+        and tokens.shape[1] == 128 * users
+        and table.shape[0] % 128 == 0
+        and negatives.shape[1] % (16 * items) == 0
+    )
+    run = functools.partial(per_device_kernels, users, items) if aligned else per_device
+    return run(tokens, lengths, destination, worker_offset, positives, negatives, table,
+               in_gain, w_uvqk, out_gain, w_out)
+
+
 def solution(mesh):
     return jax.shard_map(
-        per_device,
+        functools.partial(step, mesh.shape["user"], mesh.shape["item"]),
         mesh=mesh,
         in_specs=(
             P(("user", "item"), None),

time: 230 us -> 112 us (0.49); the launches traced: 227 us -> 111 us
  waiting for transfers between devices: 143 us -> 0 us
  Pallas kernels: 0 us -> 66.4 us
  starting transfers between devices: 21.4 us -> 0 us
  between operations: 14 us -> 0.9 us
  other arithmetic: 15.9 us -> 11.1 us
  matrix products: 18.1 us -> 21 us
  local copies, waits for them, and re-layouts: 14.7 us -> 12.2 us
    all_gather x2 -> x0, waiting for transfers between devices: 86 us -> none  [the longest x1 69.3 us: hstu_block(): lax.all_gather(w_uvqk, 'item', axis=0, tiled=True)]
    pallas_call x0 -> x2, Pallas kernels: none -> 66.4 us  [the longest x1 40.7 us: gather_all(): pl.pallas_call(functools.partial(gather_kernel, users, items), out_shape=...]
    psum x1 -> x0, waiting for transfers between devices: 45.8 us -> none  [per_device(): totals = lax.psum(row_sums.astype(jnp.bfloat16), 'user').astype(jnp.float32)]
    all_to_all x4 -> x0, starting transfers between devices: 21.3 us -> none  [the longest x1 6.46 us: dispatch(): lax.all_to_all(parcels, 'user', split_axis=0, concat_axis=0, tiled=True)]
    all_to_all x4 -> x0, waiting for transfers between devices: 9.71 us -> none  [the longest x1 6.77 us: dispatch(): lax.all_to_all(parcels, 'user', split_axis=0, concat_axis=0, tiled=True)]
    gather x4 -> x0, local copies, waits for them, and re-layouts: 8.76 us -> none  [the longest x1 2.77 us: dispatch(): rows[picked]]
    unnamed x25, local copies, waits for them, and re-layouts: 2.66 us -> 8.63 us
    select_n x6 -> x3, other arithmetic: 3.3 us -> 0.21 us  [the longest x1 0.07 us: per_device_kernels(): jnp.where(within[None, :] < counts[:, None], lower[:, None] + within[None...]
  transfers between devices with their start and end apart: 7 -> 0, of which waited for: 5 -> 0; matrix products, arithmetic and copies ran while one was open for 19% -> 0% of each run, Pallas kernels for 0% -> 0%
where the time goes in v1:
time: 112 us; the launch traced here: 111 us
  Pallas kernels  66.4 us (59%)
  matrix products  21 us (19%)
  local copies, waits for them, and re-layouts  12.2 us (11%)
  other arithmetic  11.1 us (10%)
    pallas_call x1, Pallas kernels, gather_all(): pl.pallas_call(functools.partial(gather_kernel, users, items), out_shape=...  40.7 us
    pallas_call x1, Pallas kernels, tail(): pl.pallas_call(functools.partial(tail_kernel, users, items), out_shape=(j...  25.6 us
    unnamed x25, local copies, waits for them, and re-layouts  8.63 us
    dot_general x1, matrix products, hstu_whole(): projected = jnp.dot(normed, w_full, preferred_element_type=jnp.float32)  6.73 us
    dot_general x1, matrix products, hstu_whole(): jnp.einsum('hqk,khd->qhd', weights, values_v, preferred_element_type=jnp....  3.25 us
    dot_general x1, matrix products, per_device_kernels(): owned_rows = jnp.dot(owned_pick, table_low)  2.24 us

profile of v1, /device:TPU:9, one launch (start us, length us, event | category | flops | bytes accessed | tf_op | source)
XLA Modules:
  0.0 111.5 jit_solution(5002635780448323055)
XLA Ops:
  0.6 0.8 dynamic-slice_subtract_fusion
  1.6 1.2 %fusion.20 = f32[256]{0:T(256)S(1)} fusion(bf16[256,1024]{1,0:T(8,128)(2,1)} %param.17), kind=kLoop, calls=%fused_computation.34 | loop fusion | flops 786176 | bytes 525312 | tf_op jit(solution)/shard_map/reduce_sum | solution.py:471
  2.8 2.2 %fusion.56 = bf16[256,1024]{1,0:T(8,128)(2,1)} fusion(s32[256]{0:T(256)S(1)} %eq.122, bf16[256,1024]{1,0:T(8,128)(2,1)} %param.17, f32[256]{0:T(256)S(1)} %add_rsqrt_fusion.3), kind=kOutput, calls=%fused_computation.67 | convolution fusion | flops 135069696 | bytes 1050624 | tf_op jit(solution)/shard_map/dot_general | solution.py:480
  5.0 0.8 select_reduce_fusion.2
  5.8 0.8 select_reduce_fusion.1
  6.7 0.6 broadcast_in_dim.77.l_ref
  7.4 40.7 %shard_map.130 = (bf16[4,8,32,2048]{3,2,1,0:T(8,128)(2,1)}, bf16[4,8,64,256]{3,2,1,0:T(8,128)(2,1)}, bf16[4,64,1024]{2,1,0:T(8,128)(2,1)}, s32[8,8,128]{2,1,0:T(8,128)}) custom-call(bf16[8,32,2048]{2,1,0:T(8,128)(2,1)} %bitcast.61, bf16[8,64,256]{2,1,0:T(8,128)(2,1)} %bitcast.69, bf16[4,64,1024]{2,1,0:T(8,128)(2,1)} %bitcast.60, ...), custom_call_target="tpu_custom_call" | custom-call | tf_op jit(solution)/shard_map/pallas_call | solution.py:292
  48.1 0.5 copy.31
  49.2 6.7 %multiply_convert_fusion = bf16[512,2048]{1,0:T(8,128)(2,1)} fusion(bf16[1024,2048]{1,0:T(8,128)(2,1)} %bitcast.75, bf16[512,1024]{0,1:T(8,128)(2,1)S(1)} %copy.31, f32[1024]{0:T(1024)S(1)} %copy-done.7, f32[512]{0:T(512)S(1)} %add_rsqrt_fusion.2, f32[512]{0:T(512)S(1)} %broadcast_multiply_fusion.2), kind=kOutput, calls=%fused_computation.1 | convolution fusion | flops 2155347968 | bytes 7348224 | tf_op jit(solution)/shard_map/dot_general | solution.py:417
  56.0 2.6 %slice_bitcast_fusion.1 = (bf16[64,4,8,128]{3,2,1,0:T(8,128)(2,1)}, bf16[64,4,8,128]{3,2,1,0:T(8,128)(2,1)}, bf16[512,512]{1,0:T(8,128)(2,1)S(1)}) fusion(bf16[512,2048]{1,0:T(8,128)(2,1)} %multiply_convert_fusion), kind=kLoop, calls=%fused_computation.53 | loop fusion | bytes 3145728
  58.8 0.6 fusion.74
  59.7 3.2 %fusion.75 = (f32[512]{0:T(512)S(1)}, f32[4,128,512]{2,1,0:T(8,128)S(1)}) fusion(bf16[512,4,128]{0,2,1:T(8,128)(2,1)S(1)} %bitcast.67, pred[512,512]{1,0:T(8,128)(4,1)S(1)} %fusion.31, bf16[64,4,8,128]{3,2,1,0:T(8,128)(2,1)} %get-tuple-element.34, bf16[64,4,8,128]{3,2,1,0:T(8,128)(2,1)} %get-tuple-element.33), kind=kOutput, calls=%fused_computation.117 | convolution fusion | flops 544472576 | bytes 2885632 | tf_op jit(solution)/shard_map/hqk,khd->qhd/dot_general | solution.py:431
  63.6 1.4 %multiply_convert_fusion.1 = bf16[512,512]{1,0:T(8,128)(2,1)S(1)} fusion(f32[512,512]{1,0:T(8,128)S(1)} %copy.43, bf16[512,2048]{1,0:T(8,128)(2,1)} %multiply_convert_fusion, f32[512]{0:T(512)S(1)} %copy-done.3, f32[512]{0:T(512)S(1)} %add_rsqrt_fusion.1, f32[512]{0:T(512)S(1)} %broadcast_multiply_fusion), kind=kLoop, calls=%fused_computation.39 | loop fusion | flops 1572864 | bytes 2103296 | tf_op jit(solution)/shard_map/convert_element_type | solution.py:434
  66.5 0.4 fusion.12
  67.6 0.7 fusion.13
  68.2 0.5 fusion.80
  68.7 0.7 subtract_convert_fusion
  69.4 0.8 fusion.8
  70.3 0.4 fusion.11
  70.7 1.3 %copy.39 = bf16[512,1024]{1,0:T(8,128)(2,1)} copy(bf16[512,1024]{0,1:T(8,128)(2,1)S(1)} %fusion.11) | data formatting | bytes 2097152
  72.0 0.7 fusion.33
  72.7 1.7 %convolution_add_fusion.pos_sums = f32[256,1024]{1,0:T(8,128)} fusion(f32[256,1024]{1,0:T(8,128)S(1)} %fusion.33, bf16[512,1024]{0,1:T(8,128)(2,1)S(1)} %get-tuple-element.32, f32[512]{0:T(512)S(1)} %add_rsqrt_fusion, s32[512]{0:T(512)S(1)} %broadcast_subtract_fusion, bf16[512]{0:T(512)(128)(2,1)S(1)} %get-tuple-element.29), kind=kOutput, calls=%fused_computation.27 | convolution fusion | flops 270532608 | bytes 3150848 | tf_op jit(solution)/shard_map/rc,rd->cd/dot_general | solution.py:541
  74.4 1.3 %fusion.18 = bf16[256,1024]{1,0:T(8,128)(2,1)} fusion(bf16[512,1024]{0,1:T(8,128)(2,1)S(1)} %get-tuple-element.32, f32[512]{0:T(512)S(1)} %add_rsqrt_fusion, f32[512,256]{0,1:T(8,128)S(1)} %copy-done.9, f32[512]{0:T(512)S(1)} %get-tuple-element.40, f32[512]{0:T(512)S(1)} %get-tuple-element.51), kind=kOutput, calls=%fused_computation.31 | convolution fusion | flops 270925824 | bytes 2103296 | tf_op jit(solution)/shard_map/rn,rd->nd/dot_general | solution.py:531
  75.8 1.8 %fusion.30 = bf16[512,1024]{1,0:T(8,128)(2,1)} fusion(bf16[512,1024]{0,1:T(8,128)(2,1)S(1)} %get-tuple-element.32, s32[512]{0:T(512)S(1)} %select_n.66), kind=kOutput, calls=%fused_computation.45 | convolution fusion | flops 537133056 | bytes 2099200 | tf_op jit(solution)/shard_map/dot_general | solution.py:494
  77.6 1.3 %slice_reduce_fusion.1 = (s32[8]{0:T(128)S(1)}, s32[8]{0:T(128)S(1)}) fusion(s32[8,8,128]{2,1,0:T(8,128)} %get-tuple-element.12), kind=kLoop, calls=%fused_computation.80 | loop fusion | bytes 128 | tf_op jit(solution)/shard_map/slice | solution.py:496
  79.0 0.8 fusion.49.place
  79.8 0.7 fusion.58.neg_hits
  80.5 1.1 %convert_multiply_fusion.4.table_hat = f32[256,1024]{1,0:T(8,128)} fusion(bf16[256,1024]{1,0:T(8,128)(2,1)S(1)} %copy-done, f32[256]{0:T(256)S(1)} %add_rsqrt_fusion.3), kind=kLoop, calls=%fused_computation.29 | loop fusion | flops 524288 | bytes 1573888 | tf_op jit(solution)/shard_map/mul | solution.py:472
  81.6 0.8 copy.37.table_scale
  82.4 25.6 %shard_map.131 = (bf16[256,1024]{1,0:T(8,128)(2,1)}, f32[256,128]{1,0:T(8,128)}) custom-call(bf16[8,64,1024]{2,1,0:T(8,128)(2,1)} %bitcast.62, bf16[4,64,1024]{2,1,0:T(8,128)(2,1)} %bitcast.68, f32[256,1024]{1,0:T(8,128)} %convolution_add_fusion.pos_sums, bf16[256,256]{1,0:T(8,128)(2,1)} %fusion.58.neg_hits, bf16[256,512]{1,0:T(8,128)(2,1)} %fusion.49.place, ...), custom_call_target="tpu_custom_call" | custom-call | tf_op jit(solution)/shard_map/pallas_call | solution.py:388
  108.0 1.9 %copy.62 = bf16[256,1024]{1,0:T(8,128)(2,1)} copy(bf16[256,1024]{1,0:T(8,128)(2,1)} %get-tuple-element.55) | data formatting | bytes 1048576
  109.9 1.6 %copy.63 = f32[256,128]{1,0:T(8,128)} copy(f32[256,128]{1,0:T(8,128)} %get-tuple-element.57) | data formatting | bytes 262144
  (48 shorter events, 4.3 us)
Async XLA Ops:
  0.6 47.5 %copy-start.1 = (bf16[512,1024]{1,0:T(8,128)(2,1)S(1)}, bf16[512,1024]{1,0:T(8,128)(2,1)}, u32[]{:S(2)}) copy-start(bf16[512,1024]{1,0:T(8,128)(2,1)} %param.11) | copy-start | bytes 3145732
  48.1 1.1 %copy-start.7 = (f32[1024]{0:T(1024)S(1)}, f32[1024]{0:T(1024)}, u32[]{:S(2)}) copy-start(f32[1024]{0:T(1024)} %param.18) | copy-start | bytes 12292
  56.0 2.8 %copy-start.5 = (s32[1,8]{1,0:T(1,128)S(1)}, s32[1,8]{1,0:T(1,128)}, u32[]{:S(2)}) copy-start(s32[1,8]{1,0:T(1,128)} %param.12) | copy-start | bytes 100
  62.9 0.7 copy-start.3
  63.6 1.4 %copy-start.2 = (bf16[4,8,64,256]{3,2,1,0:T(8,128)(2,1)S(1)}, bf16[4,8,64,256]{3,2,1,0:T(8,128)(2,1)}, u32[]{:S(2)}) copy-start(bf16[4,8,64,256]{3,2,1,0:T(8,128)(2,1)} %get-tuple-element.10) | copy-start | bytes 3145732
  66.5 0.7 copy-start.4
  66.5 1.0 copy-start
  67.0 1.3 %copy-start.6 = (bf16[4,64,1024]{2,1,0:T(8,128)(2,1)S(1)}, bf16[4,64,1024]{2,1,0:T(8,128)(2,1)}, u32[]{:S(2)}) copy-start(bf16[4,64,1024]{2,1,0:T(8,128)(2,1)} %get-tuple-element.11) | copy-start | bytes 1572868
  68.7 1.5 %copy-start.8 = (f32[512,256]{0,1:T(8,128)}, f32[512,256]{0,1:T(8,128)S(1)}, u32[]{:S(2)}) copy-start(f32[512,256]{0,1:T(8,128)S(1)} %get-tuple-element.46) | copy-start | bytes 1572868
  72.7 1.7 %copy-start.9 = (f32[512,256]{0,1:T(8,128)S(1)}, f32[512,256]{0,1:T(8,128)}, u32[]{:S(2)}) copy-start(f32[512,256]{0,1:T(8,128)} %copy-done.8) | copy-start | bytes 1572868

commit v2 on v0

--- a/solution.py
+++ b/solution.py
@@ -1,6 +1,10 @@
+import functools
+
 import jax
 import jax.numpy as jnp
 from jax import lax
+from jax.experimental import pallas as pl
+from jax.experimental.pallas import tpu as pltpu
 from jax.sharding import PartitionSpec as P
 
 HEAD = 128
@@ -178,9 +182,455 @@
     return (layer_out, token_grad, item_grad)
 
 
+MESH = pl.DeviceIdType.MESH
+VMEM_SPEC = pl.BlockSpec(memory_space=pltpu.VMEM)
+
+
+def remote(src, dst, send_sem, recv_sem, user, item):
+    return pltpu.make_async_remote_copy(
+        src_ref=src,
+        dst_ref=dst,
+        send_sem=send_sem,
+        recv_sem=recv_sem,
+        device_id=(user, item),
+        device_id_type=MESH,
+    )
+
+
+def greet(users, items, u, i):
+    barrier = pltpu.get_barrier_semaphore()
+    for d in range(1, users):
+        pl.semaphore_signal(
+            barrier, inc=1, device_id=(lax.rem(u + d, users), i), device_id_type=MESH
+        )
+    for d in range(1, items):
+        pl.semaphore_signal(
+            barrier, inc=1, device_id=(u, lax.rem(i + d, items)), device_id_type=MESH
+        )
+    return barrier
+
+
+def col_iota(shape):
+    return lax.broadcasted_iota(jnp.int32, shape, 1)
+
+
+def row_iota(shape):
+    return lax.broadcasted_iota(jnp.int32, shape, 0)
+
+
+def dot_f32(x, y, contract):
+    return lax.dot_general(x, y, (contract, ((), ())), preferred_element_type=jnp.float32)
+
+
+ROWS_T = ((0,), (0,))
+PLAIN = ((1,), (0,))
+COLS_T = ((1,), (1,))
+TILE = 128
+
+
+def fused_kernel(
+    users, items,
+    lens, dests, offs, tokens, pos, owned_ids, table, in_gain, w_ref, out_gain, o_ref,
+    layer_out, token_grad, item_grad,
+    wf, of, nf, lf, rows_out, labels, hat, low, scale, normed, allowed, pos_rows, pick_t,
+    acc, active, mixed, home, parcels, arrived, out_low, hi, lo, ngrad, terms, owned, sums,
+    chunks, got, inner_out, inner_got,
+    own_sem, s1, r1, s2, r2, s3, r3, sn, rn, sl, rl, sd, rd, st, rt, sc, rc, si, ri,
+):
+    f32, bf16 = jnp.float32, jnp.bfloat16
+    u = lax.axis_index("user")
+    i = lax.axis_index("item")
+    sibling = u + 1 - 2 * lax.rem(u, 2)
+    half = users // 2
+    count, width = tokens.shape
+    hist = lens.shape[1]
+    slot = count // hist
+    cat = table.shape[0]
+    share = owned_ids.shape[1] // items
+    depth = width // items
+    shard_cols = o_ref.shape[2]
+    hd = active.shape[1] // 4
+    cols = width // users
+    factor = inverse_temp / width
+    barrier = greet(users, items, u, i)
+
+    ends = []
+    total_len = jnp.int32(0)
+    starts = []
+    for h in range(hist):
+        starts.append(total_len)
+        total_len = total_len + lens[0, h]
+        ends.append(total_len)
+
+    def of_user(v, values):
+        out = jnp.int32(0)
+        for h in range(hist):
+            out = out + jnp.where(dests[0, h] == v, values[h], 0)
+        return out
+
+    for v in range(users):
+        landing = of_user(v, [offs[0, h] for h in range(hist)])
+        sent_len = of_user(v, [lens[0, h] for h in range(hist)])
+        labels[v] = jnp.where(row_iota((16, 128)) < 8, landing, sent_len)
+    t_f = table[...].astype(f32)
+    t_s = lax.rsqrt(jnp.mean(t_f * t_f, axis=1, keepdims=True) + scale_epsilon)
+    scale[...] = t_s
+    hat[...] = t_f * t_s
+    low[...] = hat[...].astype(bf16)
+    base = i * cat
+    neg_hits = (row_iota((cat, items * share)) == owned_ids[...] - base).astype(bf16)
+    rows_out[...] = dot_f32(neg_hits, low[...], ROWS_T).astype(bf16).reshape(rows_out.shape)
+
+    pl.semaphore_wait(barrier, users + items - 2)
+    pairs = ((w_ref, wf), (o_ref, of))
+    sent = []
+
+    def start(c):
+        c.start()
+        sent.append(c)
+
+    for a, (src, dst) in enumerate(pairs):
+        for d in range(1, items):
+            start(remote(src.at[u], dst.at[i, u], s1.at[a, d - 1], r1.at[a, d - 1], u, lax.rem(i + d, items)))
+    for d in range(1, items):
+        i2 = lax.rem(i + d, items)
+        start(remote(rows_out.at[i2], nf.at[i], sn.at[d - 1], rn.at[d - 1], u, i2))
+    for d in range(1, users):
+        u2 = lax.rem(u + d, users)
+        start(remote(labels.at[u2], lf.at[u], sl.at[d - 1], rl.at[d - 1], u2, i))
+    local = [
+        pltpu.make_async_copy(o_ref, of.at[i], own_sem.at[0]),
+        pltpu.make_async_copy(rows_out.at[i], nf.at[i], own_sem.at[1]),
+        pltpu.make_async_copy(labels.at[u], lf.at[u], own_sem.at[2]),
+    ]
+    for c in local:
+        c.start()
+
+    def first_hop(a, d):
+        dst = pairs[a][1]
+        i2 = lax.rem(i + items - d, items)
+        piece = dst.at[i2, u]
+        remote(piece, piece, s1.at[a, d - 1], r1.at[a, d - 1], u, i2).wait_recv()
+        for e in range(1, half):
+            start(remote(piece, piece, s2.at[a, d - 1, e - 1], r2.at[a, d - 1, e - 1], lax.rem(u + 2 * e, users), i))
+        start(remote(piece, piece, s3.at[a, d - 1, 0], r3.at[a, d - 1, 0], sibling, i))
+
+    def second_hop(a, d):
+        dst = pairs[a][1]
+        i2 = lax.rem(i + items - d, items)
+        for e in range(1, half):
+            u2 = lax.rem(u + users - 2 * e, users)
+            piece = dst.at[i2, u2]
+            remote(piece, piece, s2.at[a, d - 1, e - 1], r2.at[a, d - 1, e - 1], u2, i).wait_recv()
+            start(remote(piece, piece, s3.at[a, d - 1, e], r3.at[a, d - 1, e], sibling, i))
+
+    def last_hop(a, d):
+        dst = pairs[a][1]
+        i2 = lax.rem(i + items - d, items)
+        for e in range(half):
+            piece = dst.at[i2, lax.rem(sibling + users - 2 * e, users)]
+            remote(piece, piece, s3.at[a, d - 1, e], r3.at[a, d - 1, e], sibling, i).wait_recv()
+
+    @pl.loop(0, count // TILE)
+    def _(t):
+        rs = pl.ds(pl.multiple_of(t * TILE, TILE), TILE)
+        normed[rs, :] = layer_norm(tokens[rs, :].astype(f32), in_gain[...]).astype(bf16)
+
+    wide = 256
+
+    def project(d):
+        i2 = lax.rem(i + items - d, items)
+        x_cols = pl.ds(pl.multiple_of(i2 * depth, depth), depth)
+
+        @pl.loop(0, active.shape[1] // wide)
+        def _(t):
+            cs = pl.ds(pl.multiple_of(t * wide, wide), wide)
+            if d == 0:
+                block = w_ref[:, :, cs].reshape(depth, wide)
+            else:
+                block = wf[i2, :, :, cs].reshape(depth, wide)
+            part = dot_f32(normed[:, x_cols], block, PLAIN)
+            if d == 0:
+                acc[:, cs] = part
+            elif d < items - 1:
+                acc[:, cs] = acc[:, cs] + part
+            else:
+                active[:, cs] = jax.nn.silu(acc[:, cs] + part).astype(bf16)
+
+    def prepare_mask():
+        @pl.loop(0, count // TILE)
+        def _(t):
+            rows = row_iota((TILE, 2 * TILE)) + t * TILE
+            keys = col_iota((TILE, 2 * TILE)) + (t - 1) * TILE
+            row_seg = jnp.zeros_like(rows)
+            key_seg = jnp.zeros_like(rows)
+            for h in range(hist):
+                row_seg = row_seg + (rows >= ends[h]).astype(jnp.int32)
+                key_seg = key_seg + (keys >= ends[h]).astype(jnp.int32)
+            ok = (row_seg == key_seg) & (keys <= rows) & (keys >= 0)
+            allowed[t] = ok.astype(f32)
+
+    def prepare_positives():
+        pick_t[...] = (row_iota((cat, count)) == pos[...] - base).astype(bf16)
+
+        @pl.loop(0, count // TILE)
+        def _(t):
+            rs = pl.ds(pl.multiple_of(t * TILE, TILE), TILE)
+            pos_rows[rs, :] = dot_f32(pick_t[:, rs], low[...], ROWS_T).astype(bf16)
+
+    extra = [prepare_positives, prepare_mask]
+    project(0)
+    for d in range(1, items):
+        first_hop(0, d)
+        if extra:
+            extra.pop(0)()
+    for work in extra:
+        work()
+    second_hop(0, 1)
+    for d in range(1, items):
+        first_hop(1, d)
+    for d in range(1, items):
+        if d + 1 < items:
+            second_hop(0, d + 1)
+        last_hop(0, d)
+        project(d)
+    for d in range(1, items):
+        second_hop(1, d)
+
+    @pl.loop(0, hd // HEAD)
+    def _(h):
+        def part_of(k):
+            return pl.ds(pl.multiple_of(k * hd + h * HEAD, HEAD), HEAD)
+
+        for t in range(count // TILE):
+            first = max(t - 1, 0) * TILE
+            keys = slice(first, (t + 1) * TILE)
+            rows = slice(t * TILE, (t + 1) * TILE)
+            s = dot_f32(active[rows, part_of(2)], active[keys, part_of(3)], COLS_T) * HEAD ** (-0.5)
+            mask = allowed[t][:, 2 * TILE - s.shape[1] :]
+            wgt = jnp.where(mask > 0.5, jax.nn.silu(s), 0.0).astype(bf16)
+            mixed[rows, pl.ds(pl.multiple_of(h * HEAD, HEAD), HEAD)] = dot_f32(
+                wgt, active[keys, part_of(1)], PLAIN
+            )
+
+    for c in local:
+        c.wait()
+    for d in range(1, items):
+        last_hop(1, d)
+
+    @pl.loop(0, count // TILE)
+    def _(t):
+        rs = pl.ds(pl.multiple_of(t * TILE, TILE), TILE)
+        gated = (layer_norm(mixed[rs, :], out_gain[...]) * active[rs, :hd].astype(f32)).astype(bf16)
+        for k in range(items):
+            cs = slice(k * shard_cols, (k + 1) * shard_cols)
+            delta = dot_f32(gated, of[k].reshape(hd, shard_cols), PLAIN)
+            home[rs, cs] = (tokens[rs, cs].astype(f32) + delta).astype(bf16)
+
+    @pl.loop(0, users)
+    def _(v):
+        begin = of_user(v, starts)
+        sent_len = of_user(v, [lens[0, h] for h in range(hist)])
+        k = row_iota((slot, count))
+        pick = ((k + begin == col_iota((slot, count))) & (k < sent_len)).astype(bf16)
+        parcels[v] = dot_f32(pick, home[...], PLAIN).astype(bf16)
+
+    for d in range(1, users):
+        u2 = lax.rem(u + d, users)
+        start(remote(parcels.at[u2], arrived.at[u], sd.at[d - 1], rd.at[d - 1], u2, i))
+    mine = pltpu.make_async_copy(parcels.at[u], arrived.at[u], own_sem.at[3])
+    mine.start()
+    for d in range(1, items):
+        i2 = lax.rem(i + items - d, items)
+        remote(nf.at[i2], nf.at[i2], sn.at[d - 1], rn.at[d - 1], u, i2).wait_recv()
+
+    @pl.loop(0, count // TILE)
+    def _(t):
+        rs = pl.ds(pl.multiple_of(t * TILE, TILE), TILE)
+        group = nf[...].reshape(items * share, width)
+        out_f = home[rs, :].astype(f32)
+        out_scale = lax.rsqrt(jnp.mean(out_f * out_f, axis=1, keepdims=True) + scale_epsilon)
+        out_hat = out_f * out_scale
+        o_low = out_hat.astype(bf16)
+        out_low[rs, :] = o_low
+        o_low_f = o_low.astype(f32)
+        p_rows = pos_rows[rs, :].astype(f32)
+        pos_logit = jnp.sum(o_low_f * p_rows, axis=1, keepdims=True) * factor
+        neg_logit = dot_f32(o_low, group, COLS_T) * factor
+        pos_exp = jnp.exp(pos_logit)
+        neg_exp = jnp.exp(neg_logit)
+        partition = pos_exp + jnp.sum(neg_exp, axis=1, keepdims=True)
+        ids = row_iota((TILE, 1)) + t * TILE
+        weight = jnp.where(ids < total_len, loss_scale, 0.0)
+        pos_grad = weight * (pos_exp / partition - 1.0)
+        n_grad = (weight * neg_exp / partition).astype(bf16)
+        ngrad[rs, :] = n_grad
+        grad_hat = (pos_grad * p_rows + dot_f32(n_grad, group, PLAIN)) * factor
+        inner = jnp.mean(grad_hat * out_hat, axis=1, keepdims=True)
+        token_grad[rs, :] = ((grad_hat - out_hat * inner) * out_scale).astype(bf16)
+        pos_terms = (pos_grad * factor) * o_low_f
+        top = pos_terms.astype(bf16)
+        hi[rs, :] = top
+        lo[rs, :] = (pos_terms - top.astype(f32)).astype(bf16)
+
+    terms[...] = (dot_f32(ngrad[...], out_low[...], ROWS_T) * factor).astype(bf16).reshape(terms.shape)
+    sums[...] = dot_f32(pick_t[...], hi[...], PLAIN)
+    for d in range(1, items):
+        i2 = lax.rem(i + d, items)
+        start(remote(terms.at[i2], owned.at[i], st.at[d - 1], rt.at[d - 1], u, i2))
+    own = pltpu.make_async_copy(terms.at[i], owned.at[i], own_sem.at[4])
+    own.start()
+    sums[...] = sums[...] + dot_f32(pick_t[...], lo[...], PLAIN)
+    hits = (row_iota((cat, items * share)) == owned_ids[...] - base).astype(bf16)
+    own.wait()
+    for d in range(1, items):
+        i2 = lax.rem(i + items - d, items)
+        remote(owned.at[i2], owned.at[i2], st.at[d - 1], rt.at[d - 1], u, i2).wait_recv()
+    row_sums = sums[...] + dot_f32(hits, owned[...].reshape(items * share, width), PLAIN)
+    for v in range(users):
+        chunks[v] = row_sums[:, v * cols : (v + 1) * cols].astype(bf16)
+    inner = jnp.mean(row_sums * hat[...], axis=1, keepdims=True)
+    inner_out[...] = jnp.transpose(jnp.broadcast_to(inner, (cat, 128)))[:8]
+    for d in range(1, users):
+        u2 = lax.rem(u + d, users)
+        start(remote(chunks.at[u2], got.at[u], sc.at[d - 1], rc.at[d - 1], u2, i))
+        start(remote(inner_out, inner_got.at[u], si.at[d - 1], ri.at[d - 1], u2, i))
+    mine.wait()
+    for d in range(1, users):
+        u2 = lax.rem(u + users - d, users)
+        remote(lf.at[u2], lf.at[u2], sl.at[d - 1], rl.at[d - 1], u2, i).wait_recv()
+        remote(arrived.at[u2], arrived.at[u2], sd.at[d - 1], rd.at[d - 1], u2, i).wait_recv()
+    worker_rows = layer_out.shape[0]
+    laid = jnp.zeros((worker_rows, width), f32)
+    for v in range(0, users, 2):
+        k = col_iota((worker_rows, 2 * slot))
+        second = k >= slot
+        k = k - jnp.where(second, slot, 0)
+        begin = jnp.where(second, lf[v + 1][:1, : 2 * slot], lf[v][:1, : 2 * slot])
+        sent_len = jnp.where(second, lf[v + 1][8:9, : 2 * slot], lf[v][8:9, : 2 * slot])
+        place = ((k + begin == row_iota((worker_rows, 2 * slot))) & (k < sent_len)).astype(bf16)
+        laid = laid + dot_f32(place, arrived[v : v + 2].reshape(2 * slot, width), PLAIN)
+    layer_out[...] = laid.astype(bf16)
+    total = chunks[u].astype(f32)
+    inner_total = inner_out[...]
+    for d in range(1, users):
+        u2 = lax.rem(u + users - d, users)
+        remote(got.at[u2], got.at[u2], sc.at[d - 1], rc.at[d - 1], u2, i).wait_recv()
+        remote(inner_got.at[u2], inner_got.at[u2], si.at[d - 1], ri.at[d - 1], u2, i).wait_recv()
+        total = total + got[u2].astype(f32)
+        inner_total = inner_total + inner_got[u2]
+    inner_rows = jnp.transpose(jnp.broadcast_to(inner_total[:1], (128, cat)))
+    here = hat[:, pl.ds(pl.multiple_of(u * cols, cols), cols)]
+    item_grad[...] = (total - here * inner_rows[:, :cols]) * scale[...]
+    for c in sent:
+        c.wait_send()
+
+
+def fused(
+    users, items,
+    tokens, lengths, destination, worker_offset, positives, negatives, table,
+    in_gain, w_uvqk, out_gain, w_out,
+):
+    f32, bf16 = jnp.float32, jnp.bfloat16
+    dma = pltpu.SemaphoreType.DMA
+    half = users // 2
+    count, width = tokens.shape
+    slot = count // lengths.shape[1]
+    share = negatives.shape[1] // items
+    cat = table.shape[0]
+    cols = width // users
+    total = w_uvqk.shape[1]
+    hd = out_gain.shape[0]
+    ids = lax.dynamic_slice_in_dim(
+        negatives, lax.axis_index("item") * share, share, 1
+    ).reshape(1, -1)
+    w3 = w_uvqk.reshape(users, w_uvqk.shape[0] // users, total)
+    o3 = w_out.reshape(users, w_out.shape[0] // users, w_out.shape[1])
+    smem = pl.BlockSpec(memory_space=pltpu.SMEM)
+    return pl.pallas_call(
+        functools.partial(fused_kernel, users, items),
+        out_shape=(
+            jax.ShapeDtypeStruct((TOK_DEV, width), bf16),
+            jax.ShapeDtypeStruct((count, width), bf16),
+            jax.ShapeDtypeStruct((cat, cols), f32),
+        ),
+        in_specs=[smem] * 3 + [VMEM_SPEC] * 8,
+        out_specs=(VMEM_SPEC,) * 3,
+        scratch_shapes=[
+            pltpu.VMEM((items,) + w3.shape, bf16),
+            pltpu.VMEM((items,) + o3.shape, bf16),
+            pltpu.VMEM((items, share, width), bf16),
+            pltpu.VMEM((users, 16, 128), jnp.int32),
+            pltpu.VMEM((items, share, width), bf16),
+            pltpu.VMEM((users, 16, 128), jnp.int32),
+            pltpu.VMEM((cat, width), f32),
+            pltpu.VMEM((cat, width), bf16),
+            pltpu.VMEM((cat, 1), f32),
+            pltpu.VMEM((count, width), bf16),
+            pltpu.VMEM((count // TILE, TILE, 2 * TILE), f32),
+            pltpu.VMEM((count, width), bf16),
+            pltpu.VMEM((cat, count), bf16),
+            pltpu.VMEM((count, total), f32),
+            pltpu.VMEM((count, total), bf16),
+            pltpu.VMEM((count, hd), f32),
+            pltpu.VMEM((count, width), bf16),
+            pltpu.VMEM((users, slot, width), bf16),
+            pltpu.VMEM((users, slot, width), bf16),
+            pltpu.VMEM((count, width), bf16),
+            pltpu.VMEM((count, width), bf16),
+            pltpu.VMEM((count, width), bf16),
+            pltpu.VMEM((count, items * share), bf16),
+            pltpu.VMEM((items, share, width), bf16),
+            pltpu.VMEM((items, share, width), bf16),
+            pltpu.VMEM((cat, width), f32),
+            pltpu.VMEM((users, cat, cols), bf16),
+            pltpu.VMEM((users, cat, cols), bf16),
+            pltpu.VMEM((8, cat), f32),
+            pltpu.VMEM((users, 8, cat), f32),
+            dma((5,)),
+            dma((2, items - 1)), dma((2, items - 1)),
+            dma((2, items - 1, half - 1)), dma((2, items - 1, half - 1)),
+            dma((2, items - 1, half)), dma((2, items - 1, half)),
+            dma((items - 1,)), dma((items - 1,)),
+            dma((users - 1,)), dma((users - 1,)),
+            dma((users - 1,)), dma((users - 1,)),
+            dma((items - 1,)), dma((items - 1,)),
+            dma((users - 1,)), dma((users - 1,)),
+            dma((users - 1,)), dma((users - 1,)),
+        ],
+        compiler_params=pltpu.CompilerParams(
+            collective_id=0, has_side_effects=True, vmem_limit_bytes=60 << 20
+        ),
+    )(
+        lengths, destination, worker_offset, tokens, positives.reshape(1, -1), ids, table,
+        in_gain.reshape(1, -1), w3, out_gain.reshape(1, -1), o3,
+    )
+
+
+def step(users, items, tokens, lengths, destination, worker_offset, positives, negatives, table,
+         in_gain, w_uvqk, out_gain, w_out):
+    aligned = (
+        users % 2 == 0
+        and users > 2
+        and tokens.shape[0] % TILE == 0
+        and tokens.shape[0] // lengths.shape[1] <= TILE // 2
+        and table.shape[0] % 256 == 0
+        and items > 1
+        and w_uvqk.shape[0] % (16 * users) == 0
+        and w_out.shape[0] % (16 * users) == 0
+        and w_out.shape[1] % 128 == 0
+        and tokens.shape[1] == 128 * users
+        and table.shape[0] % 128 == 0
+        and negatives.shape[1] % (16 * items) == 0
+    )
+    run = functools.partial(fused, users, items) if aligned else per_device
+    return run(tokens, lengths, destination, worker_offset, positives, negatives, table,
+               in_gain, w_uvqk, out_gain, w_out)
+
+
 def solution(mesh):
     return jax.shard_map(
-        per_device,
+        functools.partial(step, mesh.shape["user"], mesh.shape["item"]),
         mesh=mesh,
         in_specs=(
             P(("user", "item"), None),

time: 230 us -> 78.1 us (0.34)
  the two profiles are of different devices: /device:TPU:9 before, /device:TPU:25 now
where the time goes in v2:
time: 78.1 us; the launch traced here: 77.9 us
  Pallas kernels  72.2 us (92%)
  local copies, waits for them, and re-layouts  5.04 us (6%)
    pallas_call x1, Pallas kernels, fused(): pl.pallas_call(functools.partial(fused_kernel, users, items), out_shape=(...  72.2 us
    unnamed x9, local copies, waits for them, and re-layouts  4.32 us

profile of v2, /device:TPU:25, one launch (start us, length us, event | category | flops | bytes accessed | tf_op | source)
XLA Modules:
  0.0 77.9 jit_solution(7266924243283938696)
XLA Ops:
  0.6 0.0 copy-start
  0.6 0.7 copy-done
  1.3 0.1 constant_dynamic-slice_fusion
  1.4 0.6 reshape.25.owned_ids
  2.0 72.2 %shard_map.130 = (bf16[256,1024]{1,0:T(8,128)(2,1)}, bf16[512,1024]{1,0:T(8,128)(2,1)}, f32[256,128]{1,0:T(8,128)}) custom-call(s32[1,8]{1,0:T(1,128)} %lens.1, s32[1,8]{1,0:T(1,128)} %dests.1, s32[1,8]{1,0:T(1,128)} %offs.1, bf16[512,1024]{1,0:T(8,128)(2,1)} %tokens.1, s32[1,512]{1,0:T(1,128)} %bitcast.8, s32[1,256]{1,0:T(1,128)} %reshape.25.owned_ids, ...), custom_call_target="tpu_custom_call" | custom-call | tf_op jit(solution)/shard_map/pallas_call | solution.py:550
  74.3 0.0 copy-start.1
  74.3 2.0 %copy.17 = bf16[256,1024]{1,0:T(8,128)(2,1)} copy(bf16[256,1024]{1,0:T(8,128)(2,1)} %get-tuple-element.6) | data formatting | bytes 1048576
  76.2 0.0 copy-done.1
  76.2 0.0 copy-start.2
  76.2 1.0 %copy.18 = bf16[512,1024]{1,0:T(8,128)(2,1)} copy(bf16[512,1024]{1,0:T(8,128)(2,1)S(1)} %copy-done.1) | data formatting | bytes 2097152
  77.2 0.1 copy-done.2
  77.2 0.7 copy.19
Async XLA Ops:
  0.6 0.7 copy-start
  74.3 2.0 %copy-start.1 = (bf16[512,1024]{1,0:T(8,128)(2,1)S(1)}, bf16[512,1024]{1,0:T(8,128)(2,1)}, u32[]{:S(2)}) copy-start(bf16[512,1024]{1,0:T(8,128)(2,1)} %get-tuple-element.7) | copy-start | bytes 3145732
  76.2 1.0 %copy-start.2 = (f32[256,128]{1,0:T(8,128)S(1)}, f32[256,128]{1,0:T(8,128)}, u32[]{:S(2)}) copy-start(f32[256,128]{1,0:T(8,128)} %get-tuple-element.8) | copy-start | bytes 393220

commit v3 on v2

--- a/solution.py
+++ b/solution.py
@@ -230,23 +230,28 @@
 
 def fused_kernel(
     users, items,
-    lens, dests, offs, tokens, pos, owned_ids, table, in_gain, w_ref, out_gain, o_ref,
+    lens, dests, offs, tokens, pos, negs, table, in_gain, w_ref, out_gain, o_ref,
     layer_out, token_grad, item_grad,
     wf, of, nf, lf, rows_out, labels, hat, low, scale, normed, allowed, pos_rows, pick_t,
     acc, active, mixed, home, parcels, arrived, out_low, hi, lo, ngrad, terms, owned, sums,
-    chunks, got, inner_out, inner_got,
-    own_sem, s1, r1, s2, r2, s3, r3, sn, rn, sl, rl, sd, rd, st, rt, sc, rc, si, ri,
+    chunks, got, inner_out, inner_got, kept,
+    own_sem, s1, r1, s2, r2, s3, r3, s4, r4, sn, rn, sl, rl, sd, rd, st, rt, sc, rc, si, ri,
 ):
     f32, bf16 = jnp.float32, jnp.bfloat16
     u = lax.axis_index("user")
     i = lax.axis_index("item")
-    sibling = u + 1 - 2 * lax.rem(u, 2)
     half = users // 2
+
+    def flip(v, bit):
+        return v + bit - 2 * bit * lax.rem(v // bit, 2)
+
+    sibling, near_x, near_y = flip(u, 1), flip(u, 2), flip(u, 4)
+    across = flip(near_x, 4)
     count, width = tokens.shape
     hist = lens.shape[1]
     slot = count // hist
     cat = table.shape[0]
-    share = owned_ids.shape[1] // items
+    share = negs.shape[1] // items
     depth = width // items
     shard_cols = o_ref.shape[2]
     hd = active.shape[1] // 4
@@ -278,7 +283,14 @@
     hat[...] = t_f * t_s
     low[...] = hat[...].astype(bf16)
     base = i * cat
-    neg_hits = (row_iota((cat, items * share)) == owned_ids[...] - base).astype(bf16)
+    owned_ids = []
+    for g in range(items):
+        mine_ids = negs[g : g + 1, :share]
+        for k in range(1, items):
+            mine_ids = jnp.where(i == k, negs[g : g + 1, k * share : (k + 1) * share], mine_ids)
+        owned_ids.append(mine_ids - base)
+    owned_ids = jnp.concatenate(owned_ids, axis=1)
+    neg_hits = (row_iota((cat, items * share)) == owned_ids).astype(bf16)
     rows_out[...] = dot_f32(neg_hits, low[...], ROWS_T).astype(bf16).reshape(rows_out.shape)
 
     pl.semaphore_wait(barrier, users + items - 2)
@@ -302,34 +314,49 @@
         pltpu.make_async_copy(o_ref, of.at[i], own_sem.at[0]),
         pltpu.make_async_copy(rows_out.at[i], nf.at[i], own_sem.at[1]),
         pltpu.make_async_copy(labels.at[u], lf.at[u], own_sem.at[2]),
+        pltpu.make_async_copy(w_ref, wf.at[i], own_sem.at[5]),
     ]
     for c in local:
         c.start()
 
+    def place_of(a, d, v):
+        return pairs[a][1].at[lax.rem(i + items - d, items), v]
+
+    def halves(a, d, v):
+        rows = pairs[a][1].shape[2]
+        i2 = lax.rem(i + items - d, items)
+        return [pairs[a][1].at[i2, v, : rows // 2], pairs[a][1].at[i2, v, rows // 2 :]]
+
+    def move(piece, ss, rr, a, d, e, v):
+        return remote(piece, piece, ss.at[a, d - 1, e], rr.at[a, d - 1, e], v, i)
+
     def first_hop(a, d):
-        dst = pairs[a][1]
+        piece = place_of(a, d, u)
         i2 = lax.rem(i + items - d, items)
-        piece = dst.at[i2, u]
         remote(piece, piece, s1.at[a, d - 1], r1.at[a, d - 1], u, i2).wait_recv()
-        for e in range(1, half):
-            start(remote(piece, piece, s2.at[a, d - 1, e - 1], r2.at[a, d - 1, e - 1], lax.rem(u + 2 * e, users), i))
-        start(remote(piece, piece, s3.at[a, d - 1, 0], r3.at[a, d - 1, 0], sibling, i))
+        start(move(piece, s2, r2, a, d, 0, near_x))
+        start(move(piece, s2, r2, a, d, 1, near_y))
+        start(move(piece, s3, r3, a, d, 0, sibling))
 
     def second_hop(a, d):
-        dst = pairs[a][1]
-        i2 = lax.rem(i + items - d, items)
-        for e in range(1, half):
-            u2 = lax.rem(u + users - 2 * e, users)
-            piece = dst.at[i2, u2]
-            remote(piece, piece, s2.at[a, d - 1, e - 1], r2.at[a, d - 1, e - 1], u2, i).wait_recv()
-            start(remote(piece, piece, s3.at[a, d - 1, e], r3.at[a, d - 1, e], sibling, i))
+        piece = place_of(a, d, near_x)
+        move(piece, s2, r2, a, d, 0, near_x).wait_recv()
+        start(move(halves(a, d, near_x)[0], s4, r4, a, d, 0, near_y))
+        start(move(piece, s3, r3, a, d, 1, sibling))
+        piece = place_of(a, d, near_y)
+        move(piece, s2, r2, a, d, 1, near_y).wait_recv()
+        start(move(halves(a, d, near_y)[1], s4, r4, a, d, 1, near_x))
+        start(move(piece, s3, r3, a, d, 2, sibling))
+
+    def third_hop(a, d):
+        first, second = halves(a, d, across)
+        move(first, s4, r4, a, d, 0, near_y).wait_recv()
+        move(second, s4, r4, a, d, 1, near_x).wait_recv()
+        start(move(place_of(a, d, across), s3, r3, a, d, 3, sibling))
 
     def last_hop(a, d):
-        dst = pairs[a][1]
-        i2 = lax.rem(i + items - d, items)
-        for e in range(half):
-            piece = dst.at[i2, lax.rem(sibling + users - 2 * e, users)]
-            remote(piece, piece, s3.at[a, d - 1, e], r3.at[a, d - 1, e], sibling, i).wait_recv()
+        for e, v in enumerate((sibling, flip(sibling, 2), flip(sibling, 4), flip(flip(sibling, 2), 4))):
+            move(place_of(a, d, v), s3, r3, a, d, e, sibling).wait_recv()
 
     @pl.loop(0, count // TILE)
     def _(t):
@@ -345,10 +372,7 @@
         @pl.loop(0, active.shape[1] // wide)
         def _(t):
             cs = pl.ds(pl.multiple_of(t * wide, wide), wide)
-            if d == 0:
-                block = w_ref[:, :, cs].reshape(depth, wide)
-            else:
-                block = wf[i2, :, :, cs].reshape(depth, wide)
+            block = wf[i2, :, :, cs].reshape(depth, wide)
             part = dot_f32(normed[:, x_cols], block, PLAIN)
             if d == 0:
                 acc[:, cs] = part
@@ -378,24 +402,30 @@
             rs = pl.ds(pl.multiple_of(t * TILE, TILE), TILE)
             pos_rows[rs, :] = dot_f32(pick_t[:, rs], low[...], ROWS_T).astype(bf16)
 
-    extra = [prepare_positives, prepare_mask]
+    steps = range(1, items)
+    local[3].wait()
     project(0)
-    for d in range(1, items):
+    for d in steps:
         first_hop(0, d)
-        if extra:
-            extra.pop(0)()
-    for work in extra:
-        work()
-    second_hop(0, 1)
-    for d in range(1, items):
-        first_hop(1, d)
-    for d in range(1, items):
-        if d + 1 < items:
-            second_hop(0, d + 1)
+        if d == 1:
+            prepare_positives()
+            prepare_mask()
+        else:
+            second_hop(0, d - 1)
+    first_hop(1, 1)
+    third_hop(0, 1)
+    second_hop(0, items - 1)
+    for d in steps:
+        if d > 1:
+            first_hop(1, d)
+            third_hop(0, d)
+        if d == items - 1:
+            for k in steps:
+                second_hop(1, k)
         last_hop(0, d)
         project(d)
-    for d in range(1, items):
-        second_hop(1, d)
+    for d in steps:
+        third_hop(1, d)
 
     @pl.loop(0, hd // HEAD)
     def _(h):
@@ -413,7 +443,7 @@
                 wgt, active[keys, part_of(1)], PLAIN
             )
 
-    for c in local:
+    for c in local[:3]:
         c.wait()
     for d in range(1, items):
         last_hop(1, d)
@@ -427,6 +457,37 @@
             delta = dot_f32(gated, of[k].reshape(hd, shard_cols), PLAIN)
             home[rs, cs] = (tokens[rs, cs].astype(f32) + delta).astype(bf16)
 
+    for d in range(1, items):
+        i2 = lax.rem(i + items - d, items)
+        remote(nf.at[i2], nf.at[i2], sn.at[d - 1], rn.at[d - 1], u, i2).wait_recv()
+
+    @pl.loop(0, count // TILE)
+    def _(t):
+        rs = pl.ds(pl.multiple_of(t * TILE, TILE), TILE)
+        group = nf[...].reshape(items * share, width)
+        out_f = home[rs, :].astype(f32)
+        out_scale = lax.rsqrt(jnp.mean(out_f * out_f, axis=1, keepdims=True) + scale_epsilon)
+        o_low = (out_f * out_scale).astype(bf16)
+        out_low[rs, :] = o_low
+        pos_logit = (
+            jnp.sum(o_low.astype(f32) * pos_rows[rs, :].astype(f32), axis=1, keepdims=True) * factor
+        )
+        neg_exp = jnp.exp(dot_f32(o_low, group, COLS_T) * factor)
+        pos_exp = jnp.exp(pos_logit)
+        partition = pos_exp + jnp.sum(neg_exp, axis=1, keepdims=True)
+        ids = row_iota((TILE, 1)) + t * TILE
+        weight = jnp.where(ids < total_len, loss_scale, 0.0)
+        pos_grad = weight * (pos_exp / partition - 1.0)
+        ngrad[rs, :] = (weight * neg_exp / partition).astype(bf16)
+        kept[rs, :] = jnp.where(col_iota((TILE, 128)) == 0, pos_grad, out_scale)
+
+    terms[...] = (dot_f32(ngrad[...], out_low[...], ROWS_T) * factor).astype(bf16).reshape(terms.shape)
+    for d in range(1, items):
+        i2 = lax.rem(i + d, items)
+        start(remote(terms.at[i2], owned.at[i], st.at[d - 1], rt.at[d - 1], u, i2))
+    own = pltpu.make_async_copy(terms.at[i], owned.at[i], own_sem.at[4])
+    own.start()
+
     @pl.loop(0, users)
     def _(v):
         begin = of_user(v, starts)
@@ -440,48 +501,26 @@
         start(remote(parcels.at[u2], arrived.at[u], sd.at[d - 1], rd.at[d - 1], u2, i))
     mine = pltpu.make_async_copy(parcels.at[u], arrived.at[u], own_sem.at[3])
     mine.start()
-    for d in range(1, items):
-        i2 = lax.rem(i + items - d, items)
-        remote(nf.at[i2], nf.at[i2], sn.at[d - 1], rn.at[d - 1], u, i2).wait_recv()
 
     @pl.loop(0, count // TILE)
     def _(t):
         rs = pl.ds(pl.multiple_of(t * TILE, TILE), TILE)
         group = nf[...].reshape(items * share, width)
-        out_f = home[rs, :].astype(f32)
-        out_scale = lax.rsqrt(jnp.mean(out_f * out_f, axis=1, keepdims=True) + scale_epsilon)
-        out_hat = out_f * out_scale
-        o_low = out_hat.astype(bf16)
-        out_low[rs, :] = o_low
-        o_low_f = o_low.astype(f32)
-        p_rows = pos_rows[rs, :].astype(f32)
-        pos_logit = jnp.sum(o_low_f * p_rows, axis=1, keepdims=True) * factor
-        neg_logit = dot_f32(o_low, group, COLS_T) * factor
-        pos_exp = jnp.exp(pos_logit)
-        neg_exp = jnp.exp(neg_logit)
-        partition = pos_exp + jnp.sum(neg_exp, axis=1, keepdims=True)
-        ids = row_iota((TILE, 1)) + t * TILE
-        weight = jnp.where(ids < total_len, loss_scale, 0.0)
-        pos_grad = weight * (pos_exp / partition - 1.0)
-        n_grad = (weight * neg_exp / partition).astype(bf16)
-        ngrad[rs, :] = n_grad
-        grad_hat = (pos_grad * p_rows + dot_f32(n_grad, group, PLAIN)) * factor
-        inner = jnp.mean(grad_hat * out_hat, axis=1, keepdims=True)
-        token_grad[rs, :] = ((grad_hat - out_hat * inner) * out_scale).astype(bf16)
-        pos_terms = (pos_grad * factor) * o_low_f
+        pos_grad = kept[rs, :1]
+        out_scale = kept[rs, 1:2]
+        pos_terms = (pos_grad * factor) * out_low[rs, :].astype(f32)
         top = pos_terms.astype(bf16)
         hi[rs, :] = top
         lo[rs, :] = (pos_terms - top.astype(f32)).astype(bf16)
-
-    terms[...] = (dot_f32(ngrad[...], out_low[...], ROWS_T) * factor).astype(bf16).reshape(terms.shape)
-    sums[...] = dot_f32(pick_t[...], hi[...], PLAIN)
-    for d in range(1, items):
-        i2 = lax.rem(i + d, items)
-        start(remote(terms.at[i2], owned.at[i], st.at[d - 1], rt.at[d - 1], u, i2))
-    own = pltpu.make_async_copy(terms.at[i], owned.at[i], own_sem.at[4])
-    own.start()
-    sums[...] = sums[...] + dot_f32(pick_t[...], lo[...], PLAIN)
-    hits = (row_iota((cat, items * share)) == owned_ids[...] - base).astype(bf16)
+        out_hat = home[rs, :].astype(f32) * out_scale
+        grad_hat = (
+            pos_grad * pos_rows[rs, :].astype(f32) + dot_f32(ngrad[rs, :], group, PLAIN)
+        ) * factor
+        inner = jnp.mean(grad_hat * out_hat, axis=1, keepdims=True)
+        token_grad[rs, :] = ((grad_hat - out_hat * inner) * out_scale).astype(bf16)
+
+    sums[...] = dot_f32(pick_t[...], hi[...], PLAIN) + dot_f32(pick_t[...], lo[...], PLAIN)
+    hits = (row_iota((cat, items * share)) == owned_ids).astype(bf16)
     own.wait()
     for d in range(1, items):
         i2 = lax.rem(i + items - d, items)
@@ -541,12 +580,10 @@
     cols = width // users
     total = w_uvqk.shape[1]
     hd = out_gain.shape[0]
-    ids = lax.dynamic_slice_in_dim(
-        negatives, lax.axis_index("item") * share, share, 1
-    ).reshape(1, -1)
     w3 = w_uvqk.reshape(users, w_uvqk.shape[0] // users, total)
     o3 = w_out.reshape(users, w_out.shape[0] // users, w_out.shape[1])
     smem = pl.BlockSpec(memory_space=pltpu.SMEM)
+    any_spec = pl.BlockSpec(memory_space=pl.ANY)
     return pl.pallas_call(
         functools.partial(fused_kernel, users, items),
         out_shape=(
@@ -554,7 +591,7 @@
             jax.ShapeDtypeStruct((count, width), bf16),
             jax.ShapeDtypeStruct((cat, cols), f32),
         ),
-        in_specs=[smem] * 3 + [VMEM_SPEC] * 8,
+        in_specs=[smem] * 3 + [VMEM_SPEC] * 5 + [any_spec, VMEM_SPEC, any_spec],
         out_specs=(VMEM_SPEC,) * 3,
         scratch_shapes=[
             pltpu.VMEM((items,) + w3.shape, bf16),
@@ -587,10 +624,12 @@
             pltpu.VMEM((users, cat, cols), bf16),
             pltpu.VMEM((8, cat), f32),
             pltpu.VMEM((users, 8, cat), f32),
-            dma((5,)),
+            pltpu.VMEM((count, 128), f32),
+            dma((6,)),
             dma((2, items - 1)), dma((2, items - 1)),
-            dma((2, items - 1, half - 1)), dma((2, items - 1, half - 1)),
+            dma((2, items - 1, 2)), dma((2, items - 1, 2)),
             dma((2, items - 1, half)), dma((2, items - 1, half)),
+            dma((2, items - 1, 2)), dma((2, items - 1, 2)),
             dma((items - 1,)), dma((items - 1,)),
             dma((users - 1,)), dma((users - 1,)),
             dma((users - 1,)), dma((users - 1,)),
@@ -602,7 +641,7 @@
             collective_id=0, has_side_effects=True, vmem_limit_bytes=60 << 20
         ),
     )(
-        lengths, destination, worker_offset, tokens, positives.reshape(1, -1), ids, table,
+        lengths, destination, worker_offset, tokens, positives.reshape(1, -1), negatives, table,
         in_gain.reshape(1, -1), w3, out_gain.reshape(1, -1), o3,
     )
 
@@ -611,13 +650,13 @@
          in_gain, w_uvqk, out_gain, w_out):
     aligned = (
         users % 2 == 0
-        and users > 2
+        and users == 8
         and tokens.shape[0] % TILE == 0
         and tokens.shape[0] // lengths.shape[1] <= TILE // 2
         and table.shape[0] % 256 == 0
         and items > 1
-        and w_uvqk.shape[0] % (16 * users) == 0
-        and w_out.shape[0] % (16 * users) == 0
+        and w_uvqk.shape[0] % (32 * users) == 0
+        and w_out.shape[0] % (32 * users) == 0
         and w_out.shape[1] % 128 == 0
         and tokens.shape[1] == 128 * users
         and table.shape[0] % 128 == 0

time: 78.1 us -> 76.9 us (0.985)
  the two profiles are of different devices: /device:TPU:25 before, /device:TPU:9 now
where the time goes in v3:
time: 76.9 us; the launch traced here: 76.7 us
  Pallas kernels  72.4 us (94%)
  local copies, waits for them, and re-layouts  3.64 us (5%)
    pallas_call x1, Pallas kernels, fused(): pl.pallas_call(functools.partial(fused_kernel, users, items), out_shape=(...  72.4 us
    unnamed x7, local copies, waits for them, and re-layouts  3.64 us

profile of v3, /device:TPU:9, one launch (start us, length us, event | category | flops | bytes accessed | tf_op | source)
XLA Modules:
  0.0 76.7 jit_solution(2417064192610245408)
XLA Ops:
  0.6 72.4 %shard_map.130 = (bf16[256,1024]{1,0:T(8,128)(2,1)}, bf16[512,1024]{1,0:T(8,128)(2,1)}, f32[256,128]{1,0:T(8,128)}) custom-call(s32[1,8]{1,0:T(1,128)} %lens.1, s32[1,8]{1,0:T(1,128)} %dests.1, s32[1,8]{1,0:T(1,128)} %offs.1, bf16[512,1024]{1,0:T(8,128)(2,1)} %tokens.1, s32[1,512]{1,0:T(1,128)} %bitcast.8, s32[4,256]{1,0:T(4,128)} %negs.1, ...), custom_call_target="tpu_custom_call" | custom-call | tf_op jit(solution)/shard_map/pallas_call | solution.py:587
  73.0 0.0 copy-start
  73.0 2.0 %copy.17 = bf16[256,1024]{1,0:T(8,128)(2,1)} copy(bf16[256,1024]{1,0:T(8,128)(2,1)} %get-tuple-element.6) | data formatting | bytes 1048576
  75.0 0.0 copy-done
  75.0 0.0 copy-start.1
  75.0 1.0 %copy.18 = bf16[512,1024]{1,0:T(8,128)(2,1)} copy(bf16[512,1024]{1,0:T(8,128)(2,1)S(1)} %copy-done) | data formatting | bytes 2097152
  76.0 0.1 copy-done.1
  76.0 0.7 copy.19
Async XLA Ops:
  73.0 2.0 %copy-start = (bf16[512,1024]{1,0:T(8,128)(2,1)S(1)}, bf16[512,1024]{1,0:T(8,128)(2,1)}, u32[]{:S(2)}) copy-start(bf16[512,1024]{1,0:T(8,128)(2,1)} %get-tuple-element.7) | copy-start | bytes 3145732
  75.0 1.0 %copy-start.1 = (f32[256,128]{1,0:T(8,128)S(1)}, f32[256,128]{1,0:T(8,128)}, u32[]{:S(2)}) copy-start(f32[256,128]{1,0:T(8,128)} %get-tuple-element.8) | copy-start | bytes 393220

commit v4 on v3

--- a/solution.py
+++ b/solution.py
@@ -528,11 +528,13 @@
     row_sums = sums[...] + dot_f32(hits, owned[...].reshape(items * share, width), PLAIN)
     for v in range(users):
         chunks[v] = row_sums[:, v * cols : (v + 1) * cols].astype(bf16)
+    for d in range(1, users):
+        u2 = lax.rem(u + d, users)
+        start(remote(chunks.at[u2], got.at[u], sc.at[d - 1], rc.at[d - 1], u2, i))
     inner = jnp.mean(row_sums * hat[...], axis=1, keepdims=True)
     inner_out[...] = jnp.transpose(jnp.broadcast_to(inner, (cat, 128)))[:8]
     for d in range(1, users):
         u2 = lax.rem(u + d, users)
-        start(remote(chunks.at[u2], got.at[u], sc.at[d - 1], rc.at[d - 1], u2, i))
         start(remote(inner_out, inner_got.at[u], si.at[d - 1], ri.at[d - 1], u2, i))
     mine.wait()
     for d in range(1, users):

time: 76.9 us -> 77.2 us (level)
  no operation moved by 1% of the time
where the time goes in v4:
time: 77.2 us; the launch traced here: 77 us
  Pallas kernels  72.7 us (94%)
  local copies, waits for them, and re-layouts  3.64 us (5%)
    pallas_call x1, Pallas kernels, fused(): pl.pallas_call(functools.partial(fused_kernel, users, items), out_shape=(...  72.7 us
    unnamed x7, local copies, waits for them, and re-layouts  3.64 us

profile of v4, /device:TPU:9, one launch (start us, length us, event | category | flops | bytes accessed | tf_op | source)
XLA Modules:
  0.0 77.0 jit_solution(9842442568009897468)
XLA Ops:
  0.6 72.7 %shard_map.130 = (bf16[256,1024]{1,0:T(8,128)(2,1)}, bf16[512,1024]{1,0:T(8,128)(2,1)}, f32[256,128]{1,0:T(8,128)}) custom-call(s32[1,8]{1,0:T(1,128)} %lens.1, s32[1,8]{1,0:T(1,128)} %dests.1, s32[1,8]{1,0:T(1,128)} %offs.1, bf16[512,1024]{1,0:T(8,128)(2,1)} %tokens.1, s32[1,512]{1,0:T(1,128)} %bitcast.8, s32[4,256]{1,0:T(4,128)} %negs.1, ...), custom_call_target="tpu_custom_call" | custom-call | tf_op jit(solution)/shard_map/pallas_call | solution.py:589
  73.4 0.0 copy-start
  73.4 2.0 %copy.17 = bf16[256,1024]{1,0:T(8,128)(2,1)} copy(bf16[256,1024]{1,0:T(8,128)(2,1)} %get-tuple-element.6) | data formatting | bytes 1048576
  75.3 0.0 copy-done
  75.3 0.0 copy-start.1
  75.3 1.0 %copy.18 = bf16[512,1024]{1,0:T(8,128)(2,1)} copy(bf16[512,1024]{1,0:T(8,128)(2,1)S(1)} %copy-done) | data formatting | bytes 2097152
  76.3 0.1 copy-done.1
  76.4 0.7 copy.19
Async XLA Ops:
  73.4 2.0 %copy-start = (bf16[512,1024]{1,0:T(8,128)(2,1)S(1)}, bf16[512,1024]{1,0:T(8,128)(2,1)}, u32[]{:S(2)}) copy-start(bf16[512,1024]{1,0:T(8,128)(2,1)} %get-tuple-element.7) | copy-start | bytes 3145732
  75.3 1.0 %copy-start.1 = (f32[256,128]{1,0:T(8,128)S(1)}, f32[256,128]{1,0:T(8,128)}, u32[]{:S(2)}) copy-start(f32[256,128]{1,0:T(8,128)} %get-tuple-element.8) | copy-start | bytes 393220
